TPU v7x, 256 devices: a whole 4x4x8 slice. The times are simulated.
256 devices in a mesh: ctx: 16 (over x, y), head: 16 (over z, core).
Axes of the slice: x: 4, y: 4, z: 8, core: 2. Of those that a mesh axis runs over, the one named last changes fastest.
Arguments:
- tokens: bfloat16 [16384, 4096], P('ctx', 'head'), may hold values from -6 to 6
- doc_ids: int32 [16384], P('ctx'), may hold values from 0 to 7, never falling along the last dimension, each value on 1 to 8192 neighbouring positions
- w_feat: bfloat16 [4096, 1024], P(None, 'head'), may hold values from -0.09375 to 0.09375
- w_value: bfloat16 [4096, 4096], P(None, 'head'), may hold values from -0.09375 to 0.09375
- w_window: bfloat16 [4096, 8192], P(None, 'head'), may hold values from -4 to 4
- w_out: bfloat16 [4096, 4096], P('head'), may hold values from -0.09375 to 0.09375
Outputs:
- layer_out: bfloat16 [16384, 4096], P('ctx', 'head')
Inputs may be any that keep to these rules, and one draw needn't show every extreme that they name: `doc_ids`: document ids never fall along the sequence; each of the 8 documents has 1 to 8192 tokens, and one has exactly 8192.
All inputs are finite; a program needn't handle non-finite values.
Results may differ from a plain program's by a relative error of at most 0.019.
Values may be sent and summed in bfloat16 or wider, within the bound.
A program may use at most 128 MiB of HBM per device.

v0:
```python
import jax
import jax.numpy as jnp
from jax import lax
from jax.sharding import PartitionSpec as P

HEAD_DIM = 128
FEAT = 16
WIN = 64


def entering(x, axis, join, neutral):
    place = lax.axis_index(axis)
    gathered = jax.tree.map(
        lambda a, kind: lax.all_gather(a.astype(kind), axis), x, (jnp.bfloat16, jnp.bfloat16)
    )
    state = jax.tree.map(lambda a, e: jnp.zeros_like(a) + jnp.asarray(e, a.dtype), x, neutral)

    def one(step, state):
        return join(
            state,
            jax.tree.map(
                lambda a, own: lax.dynamic_index_in_dim(a, step, 0, False).astype(own.dtype),
                gathered,
                x,
            ),
        )

    return lax.fori_loop(0, place, one, state)


def shifted(x, axis, by):
    devices = lax.axis_size(axis)
    pairs = [(i, i + by) for i in range(devices) if 0 <= i + by < devices]
    return lax.ppermute(x, axis, pairs)


def feature_map(projected):
    widened = projected.astype(jnp.float32)
    products = widened[..., :, None] * widened[..., None, :]
    products = products.reshape(widened.shape[:-1] + (FEAT * FEAT,))
    constant_term = jnp.ones(widened.shape[:-1] + (1,), jnp.float32)
    return jnp.concatenate(
        [constant_term, widened * FEAT ** (-0.25), products * (2.0 * FEAT) ** (-0.5)], -1
    ).astype(jnp.bfloat16)


def join_states(earlier, later):
    early_state, early_doc = earlier
    late_state, late_doc = later
    empty_late = late_doc[0] < 0.0
    matched = early_doc[0] == late_doc[0]
    joined = late_state + jnp.where(matched, early_state, jnp.zeros_like(early_state))
    return (jnp.where(empty_late, early_state, joined), jnp.where(empty_late, early_doc, late_doc))


def shards(tokens, doc_ids, w_feat, w_value, w_window, w_out):
    tok_rows = tokens.shape[0]
    head_count = w_value.shape[1] // HEAD_DIM
    highest = lax.Precision.HIGHEST
    zero_sums = (
        jnp.zeros((tok_rows, w_feat.shape[1]), jnp.float32),
        jnp.zeros((tok_rows, w_value.shape[1]), jnp.float32),
        jnp.zeros((tok_rows, w_window.shape[1]), jnp.float32),
    )
    column_piece = lax.all_gather(tokens, "head", axis=1, tiled=True)
    updated = []
    for running, weight in zip(zero_sums, (w_feat, w_value, w_window)):
        updated.append(jnp.dot(column_piece, weight, preferred_element_type=jnp.float32))
    feat_sum, value_sum, window_sum = tuple(updated)
    features = feat_sum.astype(jnp.bfloat16).reshape(tok_rows, head_count, 2 * FEAT)
    phi_query = feature_map(features[..., :FEAT])
    phi_key = feature_map(features[..., FEAT:])
    values_here = value_sum.astype(jnp.bfloat16).reshape(tok_rows, head_count, HEAD_DIM)
    window_proj = window_sum.astype(jnp.bfloat16).reshape(tok_rows, head_count, 2, HEAD_DIM)
    win_query = window_proj[:, :, 0]
    win_key = window_proj[:, :, 1]
    doc_float = doc_ids.astype(jnp.float32)
    positions = jnp.arange(tok_rows)
    allowed = (
        (doc_float[:, None] == doc_float[None, :]) & (positions[:, None] >= positions[None, :])
    ).astype(jnp.float32)
    scores = (
        jnp.einsum("thp,shp->hts", phi_query, phi_key, preferred_element_type=jnp.float32)
        * allowed[None]
    ).astype(jnp.bfloat16)
    inner = jnp.einsum("hts,shd->thd", scores, values_here, preferred_element_type=jnp.float32)
    keeps = doc_float == doc_float[-1]
    kept_keys = jnp.where(keeps[:, None, None], phi_key, jnp.zeros_like(phi_key))
    local_state = jnp.einsum(
        "shp,shd->hpd", kept_keys, values_here, preferred_element_type=jnp.float32
    )
    last_here = doc_float[tok_rows - 1 :]
    empty_state = jnp.zeros_like(local_state)
    incoming, in_doc = entering(
        (local_state, last_here),
        "ctx",
        join_states,
        (empty_state, jnp.full((1,), -1.0, jnp.float32)),
    )
    uses = doc_float == in_doc[0]
    carried = jnp.einsum("thp,hpd->thd", phi_query.astype(jnp.float32), incoming, precision=highest)
    linear_out = inner + jnp.where(uses[:, None, None], carried, jnp.zeros_like(carried))
    mean_square = jnp.mean(linear_out * linear_out, -1, keepdims=True)
    normed = linear_out * lax.rsqrt(mean_square + 1e-05)
    tail_key, tail_value, tail_doc = shifted(
        (
            win_key[tok_rows - WIN :],
            values_here[tok_rows - WIN :],
            (doc_float[tok_rows - WIN :] + 1.0).astype(jnp.bfloat16),
        ),
        "ctx",
        1,
    )
    keys_all = jnp.concatenate([tail_key, win_key], 0)
    values_cat = jnp.concatenate([tail_value, values_here], 0)
    docs_cat = jnp.concatenate([tail_doc.astype(jnp.float32) - 1.0, doc_float], 0)
    key_pos = jnp.arange(WIN + tok_rows)
    within = (
        (key_pos[None, :] > positions[:, None])
        & (key_pos[None, :] <= positions[:, None] + WIN)
        & (docs_cat[None, :] == doc_float[:, None])
    )
    logits = jnp.einsum(
        "thd,shd->hts", win_query, keys_all, preferred_element_type=jnp.float32
    ) * HEAD_DIM ** (-0.5)
    logits = jnp.where(within[None], logits, -1e30)
    top_logit = jnp.max(logits, -1, keepdims=True)
    weights = jnp.exp(logits - top_logit) * within[None].astype(jnp.float32)
    probs = (weights / jnp.sum(weights, -1, keepdims=True)).astype(jnp.bfloat16)
    window_out = jnp.einsum("hts,shd->thd", probs, values_cat, preferred_element_type=jnp.float32)
    mixed = (normed + window_out).astype(jnp.bfloat16).reshape(tok_rows, head_count * HEAD_DIM)
    summed = lax.psum_scatter(
        lax.dot_general(
            w_out, mixed, (((0,), (1,)), ((), ())), preferred_element_type=jnp.float32
        ).astype(jnp.bfloat16),
        "head",
        scatter_dimension=0,
        tiled=True,
    ).astype(jnp.float32)
    return summed.T.astype(jnp.bfloat16)


def solution(mesh):
    return jax.shard_map(
        shards,
        mesh=mesh,
        in_specs=(
            P("ctx", "head"),
            P("ctx"),
            P(None, "head"),
            P(None, "head"),
            P(None, "head"),
            P("head", None),
        ),
        out_specs=P("ctx", "head"),
        check_vma=False,
    )
```

profile of v0, /device:TPU:2, one launch (start us, length us, event | category | flops | bytes accessed | tf_op | source)
XLA Modules:
  0.0 281.5 jit_solution(10411707166912773014)
XLA Ops:
  8.6 1.2 dynamic-slice
  9.9 1.3 dynamic-update-slice
  11.2 3.5 %collective-permute-start.1 = (bf16[64]{0:T(256)(128)(2,1)S(1)}, bf16[64]{0:T(256)(128)(2,1)S(1)}, u32[]{:S(2)}, u32[]{:S(2)}) collective-permute-start(bf16[64]{0:T(256)(128)(2,1)S(1)} %add_convert_fusion), channel_id=1, source_target_pairs={{0,16},{16,32},{32,48},{48,64},{64,80},{80,96},{96,112},{112,128},... | collective-permute-start | bytes 392 | tf_op jit(solution)/shard_map/ppermute | solution.py:34
  14.7 33.2 %all-reduce = bf16[16]{0:T(256)(128)(2,1)S(1)} all-reduce(bf16[16]{0:T(256)(128)(2,1)S(1)} %dynamic-update-slice), channel_id=2, replica_groups=mesh['ctx'=16,'head'=16] {'ctx'}, use_global_device_ids=true, to_apply=%add | all-reduce | flops 16 | bytes 64
  48.6 1.3 broadcast_compare_fusion.1
  49.9 2.5 fusion.12
  52.4 23.7 %all-gather.5.cloned.1.call-done = bf16[1024,4096]{1,0:T(8,128)(2,1)} async-done(((bf16[1024,256]{1,0:T(8,128)(2,1)}), bf16[1024,4096]{1,0:T(8,128)(2,1)}) %all-gather.5.cloned.1.call-update) | async-done | bytes 8388624 | tf_op jit(solution)/shard_map/all_gather | solution.py:65
  76.1 6.2 %convolution_convert_fusion.3 = bf16[1024,64]{0,1:T(8,128)(2,1)S(1)} fusion(bf16[1024,4096]{1,0:T(8,128)(2,1)} %all-gather.5.cloned.1.call-done, bf16[4096,64]{0,1:T(8,128)(2,1)S(1)} %copy-done.6), kind=kOutput, calls=%fused_computation.36 | convolution fusion | flops 536936448 | bytes 9043968 | tf_op jit(solution)/shard_map/dot_general | solution.py:68
  83.9 2.3 convolution_convert_fusion.1
  87.0 1.2 convolution_convert_fusion.2
  88.4 3.5 %fusion.6 = (pred[1024,1088]{0,1:T(8,128)(4,1)}, f32[1024,1088]{0,1:T(8,128)}) fusion(f32[1024]{0:T(1024)S(1)} %convert_element_type.84, s32[1024]{0:T(1024)S(1)} %iota_add_fusion, f32[1088]{0:T(1024)S(1)} %pad_maximum_fusion.12), kind=kLoop, calls=%fused_computation.15 | loop fusion | flops 6684672 | bytes 5583104 | tf_op jit(solution)/shard_map/and | solution.py:119
  92.0 7.3 %convolution_convert_fusion = bf16[1024,512]{0,1:T(8,128)(2,1)S(1)} fusion(bf16[1024,4096]{1,0:T(8,128)(2,1)} %all-gather.5.cloned.1.call-done, bf16[4096,512]{1,0:T(8,128)(2,1)S(1)} %copy-done.10), kind=kOutput, calls=%fused_computation.26 | convolution fusion | flops 4295491584 | bytes 13631488 | tf_op jit(solution)/shard_map/dot_general | solution.py:68
  100.5 3.4 %collective-permute-start.2 = (bf16[64,2,128]{2,0,1:T(8,128)(2,1)S(1)}, bf16[64,2,128]{2,0,1:T(8,128)(2,1)S(1)}, u32[]{:S(2)}, u32[]{:S(2)}) collective-permute-start(bf16[64,2,128]{2,0,1:T(8,128)(2,1)S(1)} %bitcast.88), channel_id=1, source_target_pairs={{0,16},{16,32},{32,48},{48,64},{64,80},{80,96},{96,112},{112,128},... | collective-permute-start | bytes 98312 | tf_op jit(solution)/shard_map/ppermute | solution.py:34
  104.7 3.6 %collective-permute-start = (bf16[64,2,128]{2,0,1:T(8,128)(2,1)S(1)}, bf16[64,2,128]{2,0,1:T(8,128)(2,1)}, u32[]{:S(2)}, u32[]{:S(2)}) collective-permute-start(bf16[64,2,128]{2,0,1:T(8,128)(2,1)S(1)} %copy_bitcast_fusion.1), channel_id=1, source_target_pairs={{0,16},{16,32},{32,48},{48,64},{64,80},{80,96},{96,112},{112,128},... | collective-permute-start | bytes 98312 | tf_op jit(solution)/shard_map/ppermute | solution.py:34
  108.2 2.0 copy_bitcast_fusion
  110.2 7.8 %fusion.9 = f32[2,128,1024]{2,1,0:T(8,128)} fusion(f32[1024,1024]{1,0:T(8,128)} %fusion.12, bf16[1024,2,256]{0,2,1:T(8,128)(2,1)} %bitcast.81, bf16[1024,2,16]{0,2,1:T(8,128)(2,1)S(1)} %get-tuple-element.54, bf16[1024,2,256]{0,2,1:T(8,128)(2,1)S(1)} %bitcast.78, bf16[1024,2,16]{0,2,1:T(8,128)(2,1)S(1)} %get-tuple-element.53, ...), kind=kOutput, calls=%fused_computation.18 | convolution fusion | flops 1692819456 | bytes 7995938 | tf_op jit(solution)/shard_map/hts,shd->thd/dot_general | solution.py:86
  118.0 1.1 slice.46
  119.4 10.6 %fusion.45 = (f32[2,1024]{1,0:T(2,128)S(1)}, f32[2,1024,1088]{1,2,0:T(8,128)}) fusion(f32[1024,1088]{0,1:T(8,128)} %get-tuple-element.58, pred[1024,1088]{0,1:T(8,128)(4,1)} %get-tuple-element.57, bf16[1024,2,2,128]{0,3,2,1:T(8,128)(2,1)} %bitcast.86, bf16[1024,2,128]{2,0,1:T(8,128)(2,1)S(1)} %bitcast.82, bf16[64,2,128]{2,0,1:T(8,128)(2,1)S(1)} %collective-permute-done.2), kind=kOutput, calls=%fused_computation.77 | convolution fusion | flops 582681664 | bytes 15572992 | tf_op jit(solution)/shard_map/sub | solution.py:128
  130.0 7.5 %all-gather.7.cloned.1.call-done = bf16[32,273,128]{2,1,0:T(8,128)(2,1)} async-done(((bf16[2,273,128]{2,1,0:T(8,128)(2,1)}), bf16[32,273,128]{2,1,0:T(8,128)(2,1)}) %all-gather.7.cloned.1.call-update) | async-done | bytes 2236432 | tf_op jit(solution)/shard_map/all_gather | solution.py:14
  137.5 14.7 %while.12 = (s32[]{:T(128)}, f32[2,273,128]{2,1,0:T(8,128)S(1)}, f32[1]{0:T(128)}, s32[]{:T(128)}, bf16[16,1]{0,1:T(2,128)(2,1)S(1)}, /*index=5*/bf16[16,2,273,1...) while((s32[]{:T(128)}, f32[2,273,128]{2,1,0:T(8,128)S(1)}, f32[1]{0:T(128)}, s32[]{:T(128)}, ...), condition=%wide.region_1.2_spmd, body=%wide.region_0.1_spmd.sunk | while | flops 279560 | bytes 699054 | solution.py:28
  152.3 2.6 multiply_reduce_fusion
  154.9 4.6 %fusion.19 = bf16[1024,2,128]{0,2,1:T(8,128)(2,1)S(1)} fusion(f32[2,1024,1088]{1,2,0:T(8,128)} %get-tuple-element.60, f32[2,1024]{1,0:T(2,128)S(1)} %get-tuple-element.59, f32[1024,2,128]{0,2,1:T(8,128)S(1)} %get-tuple-element.62, bf16[1024,2,128]{2,0,1:T(8,128)(2,1)S(1)} %copy-done.7, bf16[64,2,128]{2,0,1:T(8,128)(2,1)} %collective-permute-done, ...), kind=kOutput, calls=%fused_computation.32 | convolution fusion | flops 576782336 | bytes 11059200 | tf_op jit(solution)/shard_map/hts,shd->thd/dot_general | solution.py:130
  159.5 5.6 %convert_bitcast_fusion = bf16[4096,1024]{0,1:T(8,128)(2,1)} fusion(bf16[1024,256]{0,1:T(8,128)(2,1)S(1)} %bitcast.83, bf16[256,4096]{1,0:T(8,128)(2,1)S(1)} %copy-done), kind=kOutput, calls=%fused_computation.7 | convolution fusion | flops 2151677952 | bytes 11010048 | tf_op jit(solution)/shard_map/dot_general | solution.py:133
  165.2 109.8 %reduce-scatter.2.cloned.1.call-done = bf16[256,1024]{0,1:T(8,128)(2,1)} async-done(((bf16[4096,1024]{0,1:T(8,128)(2,1)}), bf16[256,1024]{0,1:T(8,128)(2,1)}) %reduce-scatter.2.cloned.1.call-update) | async-done | bytes 524304 | tf_op jit(solution)/shard_map/reduce_scatter | solution.py:132
  (60 shorter events, 14.1 us)
Async XLA Ops:
  6.5 153.0 %copy-start = (bf16[256,4096]{1,0:T(8,128)(2,1)S(1)}, bf16[256,4096]{1,0:T(8,128)(2,1)}, u32[]{:S(2)}) copy-start(bf16[256,4096]{1,0:T(8,128)(2,1)} %param.13) | copy-start | bytes 6291460
  6.5 69.6 %copy-start.6 = (bf16[4096,64]{0,1:T(8,128)(2,1)S(1)}, bf16[4096,64]{0,1:T(8,128)(2,1)}, u32[]{:S(2)}) copy-start(bf16[4096,64]{0,1:T(8,128)(2,1)} %param.10) | copy-start | bytes 1572868
  6.5 69.6 %all-gather.5.cloned.1.call-start = ((), (), s32[]{:S(2)}) async-start(), calls=%async_computation.1 | async-start | bytes 8912896 | tf_op jit(solution)/shard_map/all_gather | solution.py:65
  7.3 130.2 %all-gather.7.cloned.1.call-start = ((), (), s32[]{:S(2)}) async-start(), calls=%async_computation.3 | async-start | bytes 2437120 | tf_op jit(solution)/shard_map/all_gather | solution.py:14
  11.2 77.1 %collective-permute-start.1 = (bf16[64]{0:T(256)(128)(2,1)S(1)}, bf16[64]{0:T(256)(128)(2,1)S(1)}, u32[]{:S(2)}, u32[]{:S(2)}) collective-permute-start(bf16[64]{0:T(256)(128)(2,1)S(1)} %add_convert_fusion), channel_id=1, source_target_pairs={{0,16},{16,32},{32,48},{48,64},{64,80},{80,96},{96,112},{112,128},... | collective-permute-start | bytes 392 | tf_op jit(solution)/shard_map/ppermute | solution.py:34
  76.1 6.8 %copy-start.1 = (bf16[1024,4096]{1,0:T(8,128)(2,1)S(1)}, bf16[1024,4096]{1,0:T(8,128)(2,1)}, u32[]{:S(2)}) copy-start(bf16[1024,4096]{1,0:T(8,128)(2,1)} %all-gather.5.cloned.1.call-done) | copy-start | bytes 25165828
  82.3 1.6 copy-start.11
  83.9 2.4 copy-start.4
  83.9 26.3 %copy-start.2 = (bf16[1024,2,16,16]{0,3,2,1:T(8,128)(2,1)}, bf16[1024,2,16,16]{0,3,2,1:T(8,128)(2,1)S(1)}, u32[]{:S(2)}) copy-start(bf16[1024,2,16,16]{0,3,2,1:T(8,128)(2,1)S(1)} %get-tuple-element.64) | copy-start | bytes 3145732
  86.2 0.8 copy-start.5
  88.3 186.7 %reduce-scatter.2.cloned.1.call-start = ((), (), s32[]{:S(2)}) async-start(), calls=%async_computation.2 | async-start | bytes 8912896 | tf_op jit(solution)/shard_map/reduce_scatter | solution.py:132
  88.4 3.5 %copy-start.10 = (bf16[4096,512]{1,0:T(8,128)(2,1)S(1)}, bf16[4096,512]{1,0:T(8,128)(2,1)}, u32[]{:S(2)}) copy-start(bf16[4096,512]{1,0:T(8,128)(2,1)} %param.12) | copy-start | bytes 12582916
  99.3 1.0 copy-start.8
  100.5 18.9 %collective-permute-start.2 = (bf16[64,2,128]{2,0,1:T(8,128)(2,1)S(1)}, bf16[64,2,128]{2,0,1:T(8,128)(2,1)S(1)}, u32[]{:S(2)}, u32[]{:S(2)}) collective-permute-start(bf16[64,2,128]{2,0,1:T(8,128)(2,1)S(1)} %bitcast.88), channel_id=1, source_target_pairs={{0,16},{16,32},{32,48},{48,64},{64,80},{80,96},{96,112},{112,128},... | collective-permute-start | bytes 98312 | tf_op jit(solution)/shard_map/ppermute | solution.py:34
  104.7 50.3 %collective-permute-start = (bf16[64,2,128]{2,0,1:T(8,128)(2,1)S(1)}, bf16[64,2,128]{2,0,1:T(8,128)(2,1)}, u32[]{:S(2)}, u32[]{:S(2)}) collective-permute-start(bf16[64,2,128]{2,0,1:T(8,128)(2,1)S(1)} %copy_bitcast_fusion.1), channel_id=1, source_target_pairs={{0,16},{16,32},{32,48},{48,64},{64,80},{80,96},{96,112},{112,128},... | collective-permute-start | bytes 98312 | tf_op jit(solution)/shard_map/ppermute | solution.py:34
  129.9 22.3 %copy-start.9 = (s32[1024]{0:T(1024)S(1)}, s32[1024]{0:T(1024)}, u32[]{:S(2)}) copy-start(s32[1024]{0:T(1024)} %param.9) | copy-start | bytes 12292
  130.0 22.3 %copy-start.3 = (bf16[1024,2,16,16]{0,3,2,1:T(8,128)(2,1)S(1)}, bf16[1024,2,16,16]{0,3,2,1:T(8,128)(2,1)}, u32[]{:S(2)}) copy-start(bf16[1024,2,16,16]{0,3,2,1:T(8,128)(2,1)} %copy-done.2) | copy-start | bytes 3145732
  152.3 2.7 copy-start.7
Sparse Core Ops, SparseCore 0:
  9.1 66.9 all-gather.4
  88.4 49.0 all-gather.6
  165.3 109.6 reduce-scatter.1
where the time goes:
time: 283 us; the launch traced here: 282 us
  waiting for transfers between devices  142 us (50%)
  matrix products  48.2 us (17%)
  blocking collectives  33.2 us (12%)
  between operations  13.4 us (5%)
  local copies, waits for them, and re-layouts  13.2 us (5%)
  other arithmetic  13.1 us (5%)
  starting transfers between devices  10.5 us (4%)
  loops' own time  8.18 us (3%)
    reduce_scatter x1, waiting for transfers between devices, shards(): lax.psum_scatter(lax.dot_general(w_out, mixed, (((0,), (1,)), ((), ())),...  110 us
    unnamed x1, blocking collectives  33.2 us
    all_gather x1, waiting for transfers between devices, shards(): column_piece = lax.all_gather(tokens, 'head', axis=1, tiled=True)  23.7 us
    dot_general x3, matrix products, shards(): jnp.dot(column_piece, weight, preferred_element_type=jnp.float32)  15.8 us
    sub x1, matrix products, shards(): weights = jnp.exp(logits - top_logit) * within[None].astype(jnp.float32)  10.6 us
    ppermute x3, starting transfers between devices, shifted(): return lax.ppermute(x, axis, pairs)  10.4 us
    another operation x1, loops' own time, entering(): return lax.fori_loop(0, place, one, state)  8.18 us
    dot_general x1, matrix products, shards(): jnp.einsum('hts,shd->thd', scores, values_here, preferred_element_type=jn...  7.79 us
  transfers between devices with their start and end apart: 6, of which 3 were waited for; matrix products, arithmetic and copies ran while one was open for 22% of the time, Pallas kernels for 0%

commit v1 on v0

v1 whole, which is shorter than its diff:
```python
import functools

import jax
import jax.numpy as jnp
import numpy as np
from jax import lax
from jax.experimental import pallas as pl
from jax.experimental.pallas import tpu as pltpu
from jax.sharding import PartitionSpec as P

HEAD_DIM = 128
FEAT = 16
WIN = 64
SUB = 256
PACKED = 160
WIDE = 256
LEAD = 128
F32 = jnp.float32
BF16 = jnp.bfloat16
MESH = pl.DeviceIdType.MESH


def selection_tables():
    first = np.zeros((FEAT, PACKED), np.float32)
    second = np.zeros((FEAT, PACKED), np.float32)
    weight = np.zeros((PACKED,), np.float32)
    for p in range(136):
        i, gap = p % 16, p // 16
        first[i, p] = 1.0
        second[(i + gap) % 16, p] = 1.0
        weight[p] = 1.0 / 32 if gap == 0 else 2.0 / 32
    for i in range(FEAT):
        first[i, 144 + i] = 1.0
        weight[144 + i] = 0.25
    query = np.zeros((2, 2, 4 * FEAT, WIDE), np.float32)
    key = np.zeros((2, 2, PACKED, 4 * FEAT), np.float32)
    pick = np.zeros((2, 2, 4 * FEAT, 128), np.float32)
    for head in range(2):
        at = head * 2 * FEAT
        query[head, 0, at : at + FEAT, :PACKED] = first * weight
        query[head, 1, at : at + FEAT, :PACKED] = second
        key[head, 0, :, at + FEAT : at + 2 * FEAT] = first.T
        key[head, 1, :, at + FEAT : at + 2 * FEAT] = second.T
        pick[head, 0, at : at + FEAT, :FEAT] = np.eye(FEAT)
        pick[head, 1, at + FEAT : at + 2 * FEAT, :FEAT] = np.eye(FEAT)
    return tuple(jnp.asarray(t, BF16) for t in (query, key, pick))


def dot(a, b):
    return lax.dot_general(a, b, (((1,), (0,)), ((), ())), preferred_element_type=F32)


def dot_nt(a, b):
    return lax.dot_general(a, b, (((1,), (1,)), ((), ())), preferred_element_type=F32)


def factor_bias(shape, dim):
    p = lax.broadcasted_iota(jnp.int32, shape, dim)
    one = jnp.where(p == 136, 1.0, 0.0)
    two = jnp.where((p == 136) | ((p >= 144) & (p < 160)), 1.0, 0.0)
    return one, two


def kernel(
    nctx, nz,
    tok, doc, wf_in, wv_in, ww_in, wo_in, query_in, key_in, pick_in,
    out,
    gath, wf, wv, ww, af, av, aw, query_t, key_t, pick_t,
    feat, wq, kcat, vcat, docc, docr, fq, fk, phiq,
    docs, lin, win, st_send, st_recv, st, mix, wo, sbuf, rbuf,
    load_sem, tok_sem, wo_sem, ring_send, ring_recv, par_send, par_recv,
    wo_send, wo_recv, doc_send, doc_recv, st_ssem, st_rsem, tail_send, tail_recv,
    mix_send, mix_recv, rs_send, rs_recv,
):
    n_sub = tok.shape[0] // SUB
    units = n_sub * nz
    rows_total = tok.shape[0]
    b = lax.axis_index("ctx")
    head = lax.axis_index("head")
    z = head // 2
    k = head - 2 * z
    other = 1 - k
    way = 1 - 2 * k
    ahead = lax.rem(z + way + nz, nz) * 2 + k
    behind = lax.rem(z - way + nz, nz) * 2 + k
    partner = z * 2 + other

    def sub_rows(i):
        return pl.ds(pl.multiple_of(i * SUB, SUB), SUB)

    def cols(block):
        return pl.ds(pl.multiple_of(block * 256, 256), 256)

    loads = [
        pltpu.make_async_copy(src, dst, load_sem.at[n])
        for n, (src, dst) in enumerate(
            [(wf_in, wf), (wv_in, wv), (ww_in, ww), (query_in, query_t), (key_in, key_t), (pick_in, pick_t)]
        )
    ]

    def tok_load(i):
        return pltpu.make_async_copy(tok.at[sub_rows(i)], gath.at[k, z, sub_rows(i)], tok_sem.at[i])

    for i in range(n_sub):
        tok_load(i).start()
    for load in loads:
        load.start()

    kcat[0:LEAD, :] = jnp.zeros((LEAD, 256), BF16)
    vcat[0:LEAD, :] = jnp.zeros((LEAD, 256), BF16)

    barrier = pltpu.get_barrier_semaphore()

    def greet(n, carry):
        pl.semaphore_signal(
            barrier, inc=1, device_id={"ctx": lax.rem(b + 1 + n, nctx)}, device_id_type=MESH
        )
        return carry

    for peer in (ahead, behind, partner):
        pl.semaphore_signal(barrier, inc=1, device_id={"head": peer}, device_id_type=MESH)
    lax.fori_loop(0, nctx - 1, greet, 0)
    af[...] = jnp.zeros_like(af)
    av[...] = jnp.zeros_like(av)
    aw[...] = jnp.zeros_like(aw)
    pl.semaphore_wait(barrier, nctx + 2)

    def ring_copy(u):
        s = u // n_sub
        rows = sub_rows(u - s * n_sub)
        src = lax.rem(z - s * way + 2 * nz, nz)
        return pltpu.make_async_remote_copy(
            src_ref=gath.at[k, src, rows],
            dst_ref=gath.at[k, src, rows],
            send_sem=ring_send.at[u],
            recv_sem=ring_recv.at[u],
            device_id={"head": ahead},
            device_id_type=MESH,
        )

    def ring_arrival(u):
        s = u // n_sub
        rows = sub_rows(u - s * n_sub)
        src = lax.rem(z - s * way + 2 * nz, nz)
        slot = gath.at[k, src, rows]
        return pltpu.make_async_remote_copy(
            src_ref=slot,
            dst_ref=slot,
            send_sem=ring_send.at[u - n_sub],
            recv_sem=ring_recv.at[u - n_sub],
            device_id={"head": ahead},
            device_id_type=MESH,
        )

    def par_copy(u, side, turn):
        s = u // n_sub
        rows = sub_rows(u - s * n_sub)
        src = lax.rem(z - s * turn + 2 * nz, nz)
        slot = gath.at[side, src, rows]
        return pltpu.make_async_remote_copy(
            src_ref=slot,
            dst_ref=slot,
            send_sem=par_send.at[u],
            recv_sem=par_recv.at[u],
            device_id={"head": partner},
            device_id_type=MESH,
        )

    def accumulate(u, side, turn):
        s = u // n_sub
        rows = sub_rows(u - s * n_sub)
        src = lax.rem(z - s * turn + 2 * nz, nz)
        x = gath[side, src, rows, :]
        w_rows = cols(src * 2 + side)
        af[rows, :] += dot(x, wf[w_rows, :])
        av[rows, :] += dot(x, wv[w_rows, :])
        aw[rows, :] += dot(x, ww[w_rows, :])

    for i in range(n_sub):
        tok_load(i).wait()
        ring_copy(i).start()
        par_copy(i, k, way).start()

    def doc_copy(c, slot):
        return pltpu.make_async_remote_copy(
            src_ref=doc,
            dst_ref=docs.at[slot],
            send_sem=doc_send.at[c],
            recv_sem=doc_recv.at[slot],
            device_id={"ctx": c},
            device_id_type=MESH,
        )

    def wo_copy(d, side, target):
        return pltpu.make_async_remote_copy(
            src_ref=wo_in.at[:, cols(d * 2 + target)],
            dst_ref=wo.at[side, d],
            send_sem=wo_send.at[d],
            recv_sem=wo_recv.at[d],
            device_id={"head": partner},
            device_id_type=MESH,
        )

    def wo_load(d):
        return pltpu.make_async_copy(wo_in.at[:, cols(d * 2 + k)], wo.at[k, d], wo_sem.at[d])

    def start_doc(c, carry):
        doc_copy(c, b).start()
        return carry

    lax.fori_loop(b + 1, nctx, start_doc, 0)

    def start_wo(d, carry):
        wo_copy(d, k, other).start()
        wo_load(d).start()
        return carry

    lax.fori_loop(0, nz, start_wo, 0)

    for load in loads:
        load.wait()

    lag = 2

    def ring_step(u, carry):
        @pl.when((u >= n_sub) & (u < units))
        def _():
            ring_arrival(u).wait_recv()

            @pl.when(u < units - n_sub)
            def _():
                ring_copy(u).start()

            par_copy(u, k, way).start()

        @pl.when(u < units)
        def _():
            accumulate(u, k, way)

        @pl.when(u >= lag)
        def _():
            par_copy(u - lag, other, -way).wait_recv()
            accumulate(u - lag, other, -way)

        return carry

    lax.fori_loop(0, units + lag, ring_step, 0)

    def round_rows(i, carry):
        rows = sub_rows(i)
        late = pl.ds(pl.multiple_of(LEAD + i * SUB, 128), SUB)
        feat[rows, :] = af[rows, :].astype(BF16)
        vcat[late, :] = av[rows, :].astype(BF16)
        wq[rows, 0:128] = aw[rows, 0:128].astype(BF16)
        kcat[late, 0:128] = aw[rows, 128:256].astype(BF16)
        wq[rows, 128:256] = aw[rows, 256:384].astype(BF16)
        kcat[late, 128:256] = aw[rows, 384:512].astype(BF16)
        return carry

    lax.fori_loop(0, n_sub, round_rows, 0)

    def tail_copy(n):
        buf = (kcat, vcat)[n]
        return pltpu.make_async_remote_copy(
            src_ref=buf.at[LEAD + rows_total - WIN : LEAD + rows_total],
            dst_ref=buf.at[LEAD - WIN : LEAD],
            send_sem=tail_send.at[n],
            recv_sem=tail_recv.at[n],
            device_id={"ctx": lax.rem(b + 1, nctx)},
            device_id_type=MESH,
        )

    mine = doc[...].astype(F32)
    first_doc = mine[0:1, 0:1]
    last_doc = mine[7:8, 127:128]
    for i in range(8):
        row = mine[i : i + 1, :]
        docr[0:1, LEAD + i * 128 : LEAD + (i + 1) * 128] = row
        docc[i * 128 : (i + 1) * 128, :] = jnp.broadcast_to(row, (128, 128)).T

    one_k, two_k = factor_bias((PACKED, 1), 0)
    keeps = docr[0:1, LEAD : LEAD + rows_total] == last_doc
    for j in range(2):
        left = dot_nt(key_t[j, 0], feat[...]) + one_k
        right = dot_nt(key_t[j, 1], feat[...]) + two_k
        phi_k = jnp.where(keeps, left * right, 0.0).astype(BF16)
        st_send[j] = dot(phi_k, vcat[LEAD : LEAD + rows_total, j * 128 : (j + 1) * 128]).astype(BF16)

    def st_copy(c, slot):
        return pltpu.make_async_remote_copy(
            src_ref=st_send,
            dst_ref=st_recv.at[slot],
            send_sem=st_ssem.at[c],
            recv_sem=st_rsem.at[slot],
            device_id={"ctx": c},
            device_id_type=MESH,
        )

    @pl.when(b < nctx - 1)
    def _():
        tail_copy(0).start()
        tail_copy(1).start()

    def start_state(c, carry):
        st_copy(c, b).start()
        return carry

    lax.fori_loop(b + 1, nctx, start_state, 0)

    one_q, two_q = factor_bias((1, WIDE), 1)

    def query_rows(i, carry):
        rows = sub_rows(i)
        x = feat[rows, :]
        for j in range(2):
            left = dot(x, query_t[j, 0]) + one_q
            right = dot(x, query_t[j, 1]) + two_q
            phiq[j, rows, :] = (left * right).astype(BF16)
            fq[j, rows, :] = dot(x, pick_t[j, 0]).astype(BF16)
            fk[j, rows, :] = dot(x, pick_t[j, 1]).astype(BF16)
        return carry

    lax.fori_loop(0, n_sub, query_rows, 0)

    for i in range(n_sub):
        lo, hi = i * SUB, (i + 1) * SUB
        t_pos = lax.broadcasted_iota(jnp.int32, (SUB, hi), 0) + lo
        s_pos = lax.broadcasted_iota(jnp.int32, (SUB, hi), 1)
        allowed = (s_pos <= t_pos) & (docc[lo:hi, 0:1] == docr[0:1, LEAD : LEAD + hi])
        for j in range(2):
            d = dot_nt(fq[j, lo:hi, :], fk[j, 0:hi, :])
            taylor = jnp.where(allowed, 1.0 + d * (0.25 + d * 0.03125), 0.0).astype(BF16)
            lin[lo:hi, j * 128 : (j + 1) * 128] = dot(
                taylor, vcat[LEAD : LEAD + hi, j * 128 : (j + 1) * 128]
            )

    def wait_doc(c, carry):
        doc_copy(b, c).wait_recv()
        return carry

    lax.fori_loop(0, b, wait_doc, 0)

    @pl.when(b == 0)
    def _():
        docr[0:1, 0:LEAD] = jnp.full((1, LEAD), -1.0, F32)

    @pl.when(b > 0)
    def _():
        tail_copy(0).wait_recv()
        tail_copy(1).wait_recv()
        docr[0:1, 0:LEAD] = docs[b - 1][7:8, :].astype(F32)

    reach = LEAD + SUB
    gap = lax.broadcasted_iota(jnp.int32, (SUB, reach), 1) - lax.broadcasted_iota(
        jnp.int32, (SUB, reach), 0
    )
    band = (gap > LEAD - WIN) & (gap <= LEAD)
    for i in range(n_sub):
        lo, hi = i * SUB, (i + 1) * SUB
        within = band & (docc[lo:hi, 0:1] == docr[0:1, lo : lo + reach])
        for j in range(2):
            at = slice(j * 128, (j + 1) * 128)
            logits = dot_nt(wq[lo:hi, at], kcat[lo : lo + reach, at]) * HEAD_DIM ** (-0.5)
            logits = jnp.where(within, logits, -1e30)
            top = jnp.max(logits, -1, keepdims=True)
            weights = jnp.where(within, jnp.exp(logits - top), 0.0)
            probs = (weights / jnp.sum(weights, -1, keepdims=True)).astype(BF16)
            win[lo:hi, at] = dot(probs, vcat[lo : lo + reach, at])

    def add_state(c, sums):
        st_copy(b, c).wait_recv()
        same = docs[c][7:8, 127:128].astype(F32) == first_doc
        return sums + jnp.where(same[None], st_recv[c].astype(F32), 0.0)

    total = lax.fori_loop(0, b, add_state, jnp.zeros((2, PACKED, 128), F32))
    st[:, 0:PACKED, :] = total.astype(BF16)
    st[:, PACKED:WIDE, :] = jnp.zeros((2, WIDE - PACKED, 128), BF16)

    def mix_copy(i, side):
        slot = mix.at[side, sub_rows(i)]
        return pltpu.make_async_remote_copy(
            src_ref=slot,
            dst_ref=slot,
            send_sem=mix_send.at[i],
            recv_sem=mix_recv.at[i],
            device_id={"head": partner},
            device_id_type=MESH,
        )

    def mix_rows(i, carry):
        rows = sub_rows(i)
        uses = docc[rows, :] == first_doc
        for j in range(2):
            at = slice(j * 128, (j + 1) * 128)
            carried = dot(phiq[j, rows, :], st[j])
            linear = lin[rows, at] + jnp.where(uses, carried, 0.0)
            square = jnp.mean(linear * linear, -1, keepdims=True)
            normed = linear * lax.rsqrt(square + 1e-5)
            mix[k, rows, at] = (normed + win[rows, at]).astype(BF16)
        mix_copy(i, k).start()
        return carry

    lax.fori_loop(0, n_sub, mix_rows, 0)

    def finish_wo(d, carry):
        wo_load(d).wait()
        wo_copy(d, other, k).wait_recv()
        return carry

    lax.fori_loop(0, nz, finish_wo, 0)

    def sum_copy(u):
        s = u // n_sub
        i = u - s * n_sub
        return pltpu.make_async_remote_copy(
            src_ref=sbuf.at[s, i],
            dst_ref=rbuf.at[s, i],
            send_sem=rs_send.at[u],
            recv_sem=rs_recv.at[u],
            device_id={"head": ahead},
            device_id_type=MESH,
        )

    def sum_step(u, carry):
        s = u // n_sub
        i = u - s * n_sub
        rows = sub_rows(i)
        dest = lax.rem(z - (s + 1) * way + 2 * nz, nz)

        @pl.when(u < n_sub)
        def _():
            mix_copy(i, other).wait_recv()

        part = dot(mix[0, rows, :], wo[0, dest]) + dot(mix[1, rows, :], wo[1, dest])

        @pl.when(u < n_sub)
        def _():
            sbuf[s, i] = part.astype(BF16)
            sum_copy(u).start()

        @pl.when(u >= n_sub)
        def _():
            sum_copy(u - n_sub).wait_recv()
            both = (part + rbuf[s - 1, i].astype(F32)).astype(BF16)

            @pl.when(u < units - n_sub)
            def _():
                sbuf[s, i] = both
                sum_copy(u).start()

            @pl.when(u >= units - n_sub)
            def _():
                out[rows, :] = both

        return carry

    lax.fori_loop(0, units, sum_step, 0)

    def drain_ring(u, carry):
        @pl.when(u < units - n_sub)
        def _():
            ring_copy(u).wait_send()
            sum_copy(u).wait_send()

        par_copy(u, k, way).wait_send()
        return carry

    lax.fori_loop(0, units, drain_ring, 0)

    def drain_later(c, carry):
        doc_copy(c, b).wait_send()
        st_copy(c, b).wait_send()
        return carry

    lax.fori_loop(b + 1, nctx, drain_later, 0)

    @pl.when(b < nctx - 1)
    def _():
        tail_copy(0).wait_send()
        tail_copy(1).wait_send()

    for i in range(n_sub):
        mix_copy(i, k).wait_send()

    def drain_wo(d, carry):
        wo_copy(d, k, other).wait_send()
        return carry

    lax.fori_loop(0, nz, drain_wo, 0)


def solution(mesh):
    nctx, nhead = mesh.shape["ctx"], mesh.shape["head"]
    nz = nhead // 2

    def shards(tokens, doc_ids, w_feat, w_value, w_window, w_out):
        rows = tokens.shape[0]
        width = w_feat.shape[0]
        n_sub = rows // SUB
        units = n_sub * nz
        dma = pltpu.SemaphoreType.DMA
        vmem = pltpu.VMEM
        any_space = pl.BlockSpec(memory_space=pl.ANY)
        vmem_space = pl.BlockSpec(memory_space=pltpu.VMEM)
        query, key, pick = selection_tables()
        return pl.pallas_call(
            functools.partial(kernel, nctx, nz),
            out_shape=jax.ShapeDtypeStruct((rows, 256), BF16),
            in_specs=[any_space, vmem_space] + [any_space] * 7,
            out_specs=vmem_space,
            scratch_shapes=[
                vmem((2, nz, rows, 256), BF16),
                vmem((width, 64), BF16),
                vmem((width, 256), BF16),
                vmem((width, 512), BF16),
                vmem((rows, 64), F32),
                vmem((rows, 256), F32),
                vmem((rows, 512), F32),
                vmem(query.shape, BF16),
                vmem(key.shape, BF16),
                vmem(pick.shape, BF16),
                vmem((rows, 64), BF16),
                vmem((rows, 256), BF16),
                vmem((LEAD + rows, 256), BF16),
                vmem((LEAD + rows, 256), BF16),
                vmem((rows, 128), F32),
                vmem((1, LEAD + rows), F32),
                vmem((2, rows, 128), BF16),
                vmem((2, rows, 128), BF16),
                vmem((2, rows, WIDE), BF16),
                vmem((nctx, 8, 128), jnp.int32),
                vmem((rows, 256), F32),
                vmem((rows, 256), F32),
                vmem((2, PACKED, 128), BF16),
                vmem((nctx, 2, PACKED, 128), BF16),
                vmem((2, WIDE, 128), BF16),
                vmem((2, rows, 256), BF16),
                vmem((2, nz, 256, 256), BF16),
                vmem((nz - 1, n_sub, SUB, 256), BF16),
                vmem((nz - 1, n_sub, SUB, 256), BF16),
                dma((6,)),
                dma((n_sub,)),
                dma((nz,)),
                dma((units,)),
                dma((units,)),
                dma((units,)),
                dma((units,)),
                dma((nz,)),
                dma((nz,)),
                dma((nctx,)),
                dma((nctx,)),
                dma((nctx,)),
                dma((nctx,)),
                dma((2,)),
                dma((2,)),
                dma((n_sub,)),
                dma((n_sub,)),
                dma((units,)),
                dma((units,)),
            ],
            compiler_params=pltpu.CompilerParams(
                collective_id=0, has_side_effects=True, vmem_limit_bytes=60 * 1024 * 1024
            ),
            name="based_layer",
        )(
            tokens,
            doc_ids.reshape(8, 128),
            w_feat,
            w_value,
            w_window,
            w_out,
            query,
            key,
            pick,
        )

    return jax.shard_map(
        shards,
        mesh=mesh,
        in_specs=(
            P("ctx", "head"),
            P("ctx"),
            P(None, "head"),
            P(None, "head"),
            P(None, "head"),
            P("head", None),
        ),
        out_specs=P("ctx", "head"),
        check_vma=False,
    )
```

time: 283 us -> 127 us (0.45)
  the two profiles are of different devices: /device:TPU:2 before, /device:TPU:30 now
where the time goes in v1:
time: 127 us
  Pallas kernels  123 us (97%)
  local copies, waits for them, and re-layouts  4.24 us (3%)
    pallas_call x1, Pallas kernels, shards(): pl.pallas_call(functools.partial(kernel, nctx, nz), out_shape=jax.ShapeDt...  123 us
    unnamed x2, local copies, waits for them, and re-layouts  4.24 us

profile of v1, /device:TPU:30, one launch (start us, length us, event | category | flops | bytes accessed | tf_op | source)
XLA Modules:
  0.0 127.2 jit_solution(5450501761449786030)
XLA Ops:
  0.0 2.4 %copy.10.wf_in = bf16[4096,64]{1,0:T(8,128)(2,1)} copy(bf16[4096,64]{0,1:T(8,128)(2,1)} %param.11) | data formatting | bytes 1048576 | tf_op args[2]
  2.4 123.0 %based_layer.1 = bf16[1024,256]{1,0:T(8,128)(2,1)} custom-call(bf16[1024,256]{1,0:T(8,128)(2,1)} %tok.1, s32[8,128]{1,0:T(8,128)} %bitcast.1, bf16[4096,64]{1,0:T(8,128)(2,1)} %copy.10.wf_in, bf16[4096,256]{1,0:T(8,128)(2,1)} %wv_in.1, bf16[4096,512]{1,0:T(8,128)(2,1)} %ww_in.1, bf16[256,4096]{1,0:T(8,128)(2,1)} %wo_in.1, ...), custom_call_target="tpu_custom_call" | custom-call | tf_op jit(solution)/shard_map/based_layer/pallas_call | solution.py:506
  125.3 1.9 %copy.12 = bf16[1024,256]{1,0:T(8,128)(2,1)} copy(bf16[1024,256]{1,0:T(8,128)(2,1)} %based_layer.1) | data formatting | bytes 1048576

commit v2 on v1

--- a/solution.py
+++ b/solution.py
@@ -12,8 +12,9 @@
 FEAT = 16
 WIN = 64
 SUB = 256
-PACKED = 160
 WIDE = 256
+PART = 32
+TABLE = 1536
 LEAD = 128
 F32 = jnp.float32
 BF16 = jnp.bfloat16
@@ -21,29 +22,38 @@
 
 
 def selection_tables():
-    first = np.zeros((FEAT, PACKED), np.float32)
-    second = np.zeros((FEAT, PACKED), np.float32)
-    weight = np.zeros((PACKED,), np.float32)
-    for p in range(136):
-        i, gap = p % 16, p // 16
-        first[i, p] = 1.0
-        second[(i + gap) % 16, p] = 1.0
-        weight[p] = 1.0 / 32 if gap == 0 else 2.0 / 32
-    for i in range(FEAT):
-        first[i, 144 + i] = 1.0
-        weight[144 + i] = 0.25
+    first = np.zeros((FEAT, WIDE), np.float32)
+    second = np.zeros((FEAT, WIDE), np.float32)
+    weight = np.zeros((WIDE,), np.float32)
+    for g in range(8):
+        for r in range(FEAT):
+            p = g * PART + r
+            first[r, p] = 1.0
+            second[(r + g) % FEAT, p] = 1.0
+            weight[p] = 1.0 / 32 if g == 0 else 2.0 / 32
+        p = g * PART + 16
+        first[g, p] = 1.0
+        second[g + 8, p] = 1.0
+        weight[p] = 2.0 / 32
+        for n in range(2):
+            first[2 * g + n, p + 1 + n] = 1.0
+            weight[p + 1 + n] = 0.25
     query = np.zeros((2, 2, 4 * FEAT, WIDE), np.float32)
-    key = np.zeros((2, 2, PACKED, 4 * FEAT), np.float32)
+    key = np.zeros((2, 2, WIDE, 4 * FEAT), np.float32)
     pick = np.zeros((2, 2, 4 * FEAT, 128), np.float32)
     for head in range(2):
         at = head * 2 * FEAT
-        query[head, 0, at : at + FEAT, :PACKED] = first * weight
-        query[head, 1, at : at + FEAT, :PACKED] = second
+        query[head, 0, at : at + FEAT] = first * weight
+        query[head, 1, at : at + FEAT] = second
         key[head, 0, :, at + FEAT : at + 2 * FEAT] = first.T
         key[head, 1, :, at + FEAT : at + 2 * FEAT] = second.T
         pick[head, 0, at : at + FEAT, :FEAT] = np.eye(FEAT)
         pick[head, 1, at + FEAT : at + 2 * FEAT, :FEAT] = np.eye(FEAT)
-    return tuple(jnp.asarray(t, BF16) for t in (query, key, pick))
+    table = np.zeros((TABLE, WIDE), np.float32)
+    table[0:256] = query.reshape(256, WIDE)
+    table[256:1280, 0 : 4 * FEAT] = key.reshape(4 * WIDE, 4 * FEAT)
+    table[1280:1536, 0:128] = pick.reshape(256, 128)
+    return jnp.asarray(table, BF16)
 
 
 def dot(a, b):
@@ -56,25 +66,26 @@
 
 def factor_bias(shape, dim):
     p = lax.broadcasted_iota(jnp.int32, shape, dim)
-    one = jnp.where(p == 136, 1.0, 0.0)
-    two = jnp.where((p == 136) | ((p >= 144) & (p < 160)), 1.0, 0.0)
+    one = jnp.where(p == 19, 1.0, 0.0)
+    two = jnp.where((p == 19) | (p % PART == 17) | (p % PART == 18), 1.0, 0.0)
     return one, two
 
 
 def kernel(
     nctx, nz,
-    tok, doc, wf_in, wv_in, ww_in, wo_in, query_in, key_in, pick_in,
+    tok, doc, wf_in, wv_in, ww_in, wo_in, table_in,
     out,
-    gath, wf, wv, ww, af, av, aw, query_t, key_t, pick_t,
+    gath, wf, wv, ww, af, av, aw, table,
     feat, wq, kcat, vcat, docc, docr, fq, fk, phiq,
-    docs, lin, win, st_send, st_recv, st, mix, wo, sbuf, rbuf,
+    docs, lin, win, st_send, st_recv, st_sums, st, mix, wo, sbuf, rbuf,
     load_sem, tok_sem, wo_sem, ring_send, ring_recv, par_send, par_recv,
-    wo_send, wo_recv, doc_send, doc_recv, st_ssem, st_rsem, tail_send, tail_recv,
+    wo_send, wo_recv, doc_send, doc_recv, st_ssem, st_rsem, sum_ssem, sum_rsem, tail_send, tail_recv,
     mix_send, mix_recv, rs_send, rs_recv,
 ):
     n_sub = tok.shape[0] // SUB
     units = n_sub * nz
     rows_total = tok.shape[0]
+    part = WIDE // nctx
     b = lax.axis_index("ctx")
     head = lax.axis_index("head")
     z = head // 2
@@ -91,10 +102,13 @@
     def cols(block):
         return pl.ds(pl.multiple_of(block * 256, 256), 256)
 
+    def bulk(ref, sem):
+        return pltpu.make_async_copy(ref, ref, sem.at[0])
+
     loads = [
         pltpu.make_async_copy(src, dst, load_sem.at[n])
         for n, (src, dst) in enumerate(
-            [(wf_in, wf), (wv_in, wv), (ww_in, ww), (query_in, query_t), (key_in, key_t), (pick_in, pick_t)]
+            [(wf_in, wf), (wv_in, wv), (ww_in, ww), (table_in, table)]
         )
     ]
 
@@ -132,7 +146,7 @@
         return pltpu.make_async_remote_copy(
             src_ref=gath.at[k, src, rows],
             dst_ref=gath.at[k, src, rows],
-            send_sem=ring_send.at[u],
+            send_sem=ring_send.at[0],
             recv_sem=ring_recv.at[u],
             device_id={"head": ahead},
             device_id_type=MESH,
@@ -146,7 +160,7 @@
         return pltpu.make_async_remote_copy(
             src_ref=slot,
             dst_ref=slot,
-            send_sem=ring_send.at[u - n_sub],
+            send_sem=ring_send.at[0],
             recv_sem=ring_recv.at[u - n_sub],
             device_id={"head": ahead},
             device_id_type=MESH,
@@ -160,7 +174,7 @@
         return pltpu.make_async_remote_copy(
             src_ref=slot,
             dst_ref=slot,
-            send_sem=par_send.at[u],
+            send_sem=par_send.at[0],
             recv_sem=par_recv.at[u],
             device_id={"head": partner},
             device_id_type=MESH,
@@ -172,7 +186,7 @@
         src = lax.rem(z - s * turn + 2 * nz, nz)
         x = gath[side, src, rows, :]
         w_rows = cols(src * 2 + side)
-        af[rows, :] += dot(x, wf[w_rows, :])
+        af[rows, :] += dot_nt(x, wf[:, w_rows])
         av[rows, :] += dot(x, wv[w_rows, :])
         aw[rows, :] += dot(x, ww[w_rows, :])
 
@@ -185,8 +199,8 @@
         return pltpu.make_async_remote_copy(
             src_ref=doc,
             dst_ref=docs.at[slot],
-            send_sem=doc_send.at[c],
-            recv_sem=doc_recv.at[slot],
+            send_sem=doc_send.at[0],
+            recv_sem=doc_recv.at[0],
             device_id={"ctx": c},
             device_id_type=MESH,
         )
@@ -195,20 +209,20 @@
         return pltpu.make_async_remote_copy(
             src_ref=wo_in.at[:, cols(d * 2 + target)],
             dst_ref=wo.at[side, d],
-            send_sem=wo_send.at[d],
-            recv_sem=wo_recv.at[d],
+            send_sem=wo_send.at[0],
+            recv_sem=wo_recv.at[0],
             device_id={"head": partner},
             device_id_type=MESH,
         )
 
     def wo_load(d):
-        return pltpu.make_async_copy(wo_in.at[:, cols(d * 2 + k)], wo.at[k, d], wo_sem.at[d])
-
-    def start_doc(c, carry):
-        doc_copy(c, b).start()
-        return carry
-
-    lax.fori_loop(b + 1, nctx, start_doc, 0)
+        return pltpu.make_async_copy(wo_in.at[:, cols(d * 2 + k)], wo.at[k, d], wo_sem.at[0])
+
+    def start_doc(n, carry):
+        doc_copy(lax.rem(b + n, nctx), b).start()
+        return carry
+
+    lax.fori_loop(1, nctx, start_doc, 0)
 
     def start_wo(d, carry):
         wo_copy(d, k, other).start()
@@ -271,41 +285,42 @@
         )
 
     mine = doc[...].astype(F32)
-    first_doc = mine[0:1, 0:1]
     last_doc = mine[7:8, 127:128]
     for i in range(8):
         row = mine[i : i + 1, :]
         docr[0:1, LEAD + i * 128 : LEAD + (i + 1) * 128] = row
         docc[i * 128 : (i + 1) * 128, :] = jnp.broadcast_to(row, (128, 128)).T
 
-    one_k, two_k = factor_bias((PACKED, 1), 0)
+    one_k, two_k = factor_bias((WIDE, 1), 0)
     keeps = docr[0:1, LEAD : LEAD + rows_total] == last_doc
     for j in range(2):
-        left = dot_nt(key_t[j, 0], feat[...]) + one_k
-        right = dot_nt(key_t[j, 1], feat[...]) + two_k
+        at = 256 + 512 * j
+        left = dot_nt(table[at : at + 256, 0:64], feat[...]) + one_k
+        right = dot_nt(table[at + 256 : at + 512, 0:64], feat[...]) + two_k
         phi_k = jnp.where(keeps, left * right, 0.0).astype(BF16)
-        st_send[j] = dot(phi_k, vcat[LEAD : LEAD + rows_total, j * 128 : (j + 1) * 128]).astype(BF16)
+        local = dot(phi_k, vcat[LEAD : LEAD + rows_total, j * 128 : (j + 1) * 128])
+        st_send[:, j * part : (j + 1) * part, :] = local.astype(BF16).reshape(nctx, part, 128)
 
     def st_copy(c, slot):
         return pltpu.make_async_remote_copy(
-            src_ref=st_send,
+            src_ref=st_send.at[c],
             dst_ref=st_recv.at[slot],
-            send_sem=st_ssem.at[c],
-            recv_sem=st_rsem.at[slot],
+            send_sem=st_ssem.at[0],
+            recv_sem=st_rsem.at[0],
             device_id={"ctx": c},
             device_id_type=MESH,
         )
+
+    def start_state(n, carry):
+        st_copy(lax.rem(b + n, nctx), b).start()
+        return carry
+
+    lax.fori_loop(1, nctx, start_state, 0)
 
     @pl.when(b < nctx - 1)
     def _():
         tail_copy(0).start()
         tail_copy(1).start()
-
-    def start_state(c, carry):
-        st_copy(c, b).start()
-        return carry
-
-    lax.fori_loop(b + 1, nctx, start_state, 0)
 
     one_q, two_q = factor_bias((1, WIDE), 1)
 
@@ -313,11 +328,12 @@
         rows = sub_rows(i)
         x = feat[rows, :]
         for j in range(2):
-            left = dot(x, query_t[j, 0]) + one_q
-            right = dot(x, query_t[j, 1]) + two_q
+            left = dot(x, table[128 * j : 128 * j + 64, :]) + one_q
+            right = dot(x, table[128 * j + 64 : 128 * j + 128, :]) + two_q
             phiq[j, rows, :] = (left * right).astype(BF16)
-            fq[j, rows, :] = dot(x, pick_t[j, 0]).astype(BF16)
-            fk[j, rows, :] = dot(x, pick_t[j, 1]).astype(BF16)
+            at = 1280 + 128 * j
+            fq[j, rows, :] = dot(x, table[at : at + 64, 0:128]).astype(BF16)
+            fk[j, rows, :] = dot(x, table[at + 64 : at + 128, 0:128]).astype(BF16)
         return carry
 
     lax.fori_loop(0, n_sub, query_rows, 0)
@@ -334,11 +350,36 @@
                 taylor, vcat[LEAD : LEAD + hi, j * 128 : (j + 1) * 128]
             )
 
-    def wait_doc(c, carry):
-        doc_copy(b, c).wait_recv()
-        return carry
-
-    lax.fori_loop(0, b, wait_doc, 0)
+    def sum_back(c, slot):
+        return pltpu.make_async_remote_copy(
+            src_ref=st_sums.at[c],
+            dst_ref=st.at[slot],
+            send_sem=sum_ssem.at[0],
+            recv_sem=sum_rsem.at[0],
+            device_id={"ctx": c},
+            device_id_type=MESH,
+        )
+
+    bulk(docs.at[0 : nctx - 1], doc_recv).wait()
+    bulk(st_recv.at[0 : nctx - 1], st_rsem).wait()
+    docs[b] = doc[...]
+    st_recv[b] = st_send[b]
+
+    def add_block(c, carry):
+        sums, sums_doc = carry
+        block_doc = docs[c][7:8, 127:128]
+        sums = st_recv[c].astype(F32) + jnp.where(sums_doc == block_doc, sums, 0.0)
+        st_sums[c + 1] = sums.astype(BF16)
+
+        @pl.when(c + 1 != b)
+        def _():
+            sum_back(c + 1, b).start()
+
+        return sums, block_doc
+
+    lax.fori_loop(
+        0, nctx - 1, add_block, (jnp.zeros((2 * part, 128), F32), jnp.full((1, 1), -1, jnp.int32))
+    )
 
     @pl.when(b == 0)
     def _():
@@ -367,21 +408,25 @@
             probs = (weights / jnp.sum(weights, -1, keepdims=True)).astype(BF16)
             win[lo:hi, at] = dot(probs, vcat[lo : lo + reach, at])
 
-    def add_state(c, sums):
-        st_copy(b, c).wait_recv()
-        same = docs[c][7:8, 127:128].astype(F32) == first_doc
-        return sums + jnp.where(same[None], st_recv[c].astype(F32), 0.0)
-
-    total = lax.fori_loop(0, b, add_state, jnp.zeros((2, PACKED, 128), F32))
-    st[:, 0:PACKED, :] = total.astype(BF16)
-    st[:, PACKED:WIDE, :] = jnp.zeros((2, WIDE - PACKED, 128), BF16)
+    @pl.when(b == 0)
+    def _():
+        st[...] = jnp.zeros_like(st)
+
+    @pl.when(b > 0)
+    def _():
+        bulk(st.at[0 : nctx - 1], sum_rsem).wait()
+        st[b] = st_sums[b]
+
+    state = [
+        st[:, j * part : (j + 1) * part, :].reshape(WIDE, 128) for j in range(2)
+    ]
 
     def mix_copy(i, side):
         slot = mix.at[side, sub_rows(i)]
         return pltpu.make_async_remote_copy(
             src_ref=slot,
             dst_ref=slot,
-            send_sem=mix_send.at[i],
+            send_sem=mix_send.at[0],
             recv_sem=mix_recv.at[i],
             device_id={"head": partner},
             device_id_type=MESH,
@@ -389,10 +434,10 @@
 
     def mix_rows(i, carry):
         rows = sub_rows(i)
-        uses = docc[rows, :] == first_doc
+        uses = docc[rows, :] == docr[0:1, LEAD - 1 : LEAD]
         for j in range(2):
             at = slice(j * 128, (j + 1) * 128)
-            carried = dot(phiq[j, rows, :], st[j])
+            carried = dot(phiq[j, rows, :], state[j])
             linear = lin[rows, at] + jnp.where(uses, carried, 0.0)
             square = jnp.mean(linear * linear, -1, keepdims=True)
             normed = linear * lax.rsqrt(square + 1e-5)
@@ -400,14 +445,9 @@
         mix_copy(i, k).start()
         return carry
 
-    lax.fori_loop(0, n_sub, mix_rows, 0)
-
-    def finish_wo(d, carry):
-        wo_load(d).wait()
-        wo_copy(d, other, k).wait_recv()
-        return carry
-
-    lax.fori_loop(0, nz, finish_wo, 0)
+
+    bulk(wo.at[k], wo_sem).wait()
+    bulk(wo.at[other], wo_recv).wait()
 
     def sum_copy(u):
         s = u // n_sub
@@ -415,7 +455,7 @@
         return pltpu.make_async_remote_copy(
             src_ref=sbuf.at[s, i],
             dst_ref=rbuf.at[s, i],
-            send_sem=rs_send.at[u],
+            send_sem=rs_send.at[0],
             recv_sem=rs_recv.at[u],
             device_id={"head": ahead},
             device_id_type=MESH,
@@ -454,39 +494,40 @@
 
         return carry
 
-    lax.fori_loop(0, units, sum_step, 0)
-
-    def drain_ring(u, carry):
-        @pl.when(u < units - n_sub)
-        def _():
-            ring_copy(u).wait_send()
-            sum_copy(u).wait_send()
-
-        par_copy(u, k, way).wait_send()
-        return carry
-
-    lax.fori_loop(0, units, drain_ring, 0)
-
-    def drain_later(c, carry):
-        doc_copy(c, b).wait_send()
-        st_copy(c, b).wait_send()
-        return carry
-
-    lax.fori_loop(b + 1, nctx, drain_later, 0)
+    def first_step(i, carry):
+        @pl.when(i < n_sub)
+        def _():
+            mix_rows(i, 0)
+
+        @pl.when(i > 0)
+        def _():
+            sum_step(i - 1, 0)
+
+        return carry
+
+    lax.fori_loop(0, n_sub + 1, first_step, 0)
+    lax.fori_loop(n_sub, units, sum_step, 0)
+
+    bulk(gath.at[k, 0 : nz - 1], ring_send).wait()
+    bulk(gath.at[k], par_send).wait()
+    bulk(sbuf, rs_send).wait()
+    bulk(docs.at[0 : nctx - 1], doc_send).wait()
+    bulk(st_send.at[0 : nctx - 1], st_ssem).wait()
+    bulk(mix.at[k], mix_send).wait()
+    bulk(wo.at[k], wo_send).wait()
+
+    @pl.when(b == 0)
+    def _():
+        bulk(st_sums.at[0 : nctx - 1], sum_ssem).wait()
+
+    @pl.when(b > 0)
+    def _():
+        bulk(st_sums.at[0 : nctx - 2], sum_ssem).wait()
 
     @pl.when(b < nctx - 1)
     def _():
         tail_copy(0).wait_send()
         tail_copy(1).wait_send()
-
-    for i in range(n_sub):
-        mix_copy(i, k).wait_send()
-
-    def drain_wo(d, carry):
-        wo_copy(d, k, other).wait_send()
-        return carry
-
-    lax.fori_loop(0, nz, drain_wo, 0)
 
 
 def solution(mesh):
@@ -495,30 +536,27 @@
 
     def shards(tokens, doc_ids, w_feat, w_value, w_window, w_out):
         rows = tokens.shape[0]
-        width = w_feat.shape[0]
+        width = w_value.shape[0]
         n_sub = rows // SUB
         units = n_sub * nz
         dma = pltpu.SemaphoreType.DMA
         vmem = pltpu.VMEM
-        any_space = pl.BlockSpec(memory_space=pl.ANY)
+        hbm_space = pl.BlockSpec(memory_space=pltpu.HBM)
         vmem_space = pl.BlockSpec(memory_space=pltpu.VMEM)
-        query, key, pick = selection_tables()
         return pl.pallas_call(
             functools.partial(kernel, nctx, nz),
             out_shape=jax.ShapeDtypeStruct((rows, 256), BF16),
-            in_specs=[any_space, vmem_space] + [any_space] * 7,
+            in_specs=[hbm_space, vmem_space] + [hbm_space] * 5,
             out_specs=vmem_space,
             scratch_shapes=[
                 vmem((2, nz, rows, 256), BF16),
-                vmem((width, 64), BF16),
+                vmem((64, width), BF16),
                 vmem((width, 256), BF16),
                 vmem((width, 512), BF16),
                 vmem((rows, 64), F32),
                 vmem((rows, 256), F32),
                 vmem((rows, 512), F32),
-                vmem(query.shape, BF16),
-                vmem(key.shape, BF16),
-                vmem(pick.shape, BF16),
+                vmem((TABLE, WIDE), BF16),
                 vmem((rows, 64), BF16),
                 vmem((rows, 256), BF16),
                 vmem((LEAD + rows, 256), BF16),
@@ -531,47 +569,48 @@
                 vmem((nctx, 8, 128), jnp.int32),
                 vmem((rows, 256), F32),
                 vmem((rows, 256), F32),
-                vmem((2, PACKED, 128), BF16),
-                vmem((nctx, 2, PACKED, 128), BF16),
-                vmem((2, WIDE, 128), BF16),
+                vmem((nctx, 2 * WIDE // nctx, 128), BF16),
+                vmem((nctx, 2 * WIDE // nctx, 128), BF16),
+                vmem((nctx, 2 * WIDE // nctx, 128), BF16),
+                vmem((nctx, 2 * WIDE // nctx, 128), BF16),
                 vmem((2, rows, 256), BF16),
                 vmem((2, nz, 256, 256), BF16),
                 vmem((nz - 1, n_sub, SUB, 256), BF16),
                 vmem((nz - 1, n_sub, SUB, 256), BF16),
-                dma((6,)),
+                dma((4,)),
                 dma((n_sub,)),
-                dma((nz,)),
+                dma((1,)),
+                dma((1,)),
                 dma((units,)),
+                dma((1,)),
                 dma((units,)),
-                dma((units,)),
-                dma((units,)),
-                dma((nz,)),
-                dma((nz,)),
-                dma((nctx,)),
-                dma((nctx,)),
-                dma((nctx,)),
-                dma((nctx,)),
+                dma((1,)),
+                dma((1,)),
+                dma((1,)),
+                dma((1,)),
+                dma((1,)),
+                dma((1,)),
+                dma((1,)),
+                dma((1,)),
                 dma((2,)),
                 dma((2,)),
+                dma((1,)),
                 dma((n_sub,)),
-                dma((n_sub,)),
-                dma((units,)),
+                dma((1,)),
                 dma((units,)),
             ],
             compiler_params=pltpu.CompilerParams(
-                collective_id=0, has_side_effects=True, vmem_limit_bytes=60 * 1024 * 1024
+                collective_id=0, has_side_effects=True, vmem_limit_bytes=67043328 - 600 * 1024
             ),
             name="based_layer",
         )(
             tokens,
             doc_ids.reshape(8, 128),
-            w_feat,
+            w_feat.T,
             w_value,
             w_window,
             w_out,
-            query,
-            key,
-            pick,
+            selection_tables(),
         )
 
     return jax.shard_map(

time: 127 us -> 113 us (0.89)
  the two profiles are of different devices: /device:TPU:30 before, /device:TPU:2 now
where the time goes in v2:
time: 113 us; the launch traced here: 112 us
  Pallas kernels  110 us (97%)
  local copies, waits for them, and re-layouts  1.87 us (2%)
    pallas_call x1, Pallas kernels, shards(): pl.pallas_call(functools.partial(kernel, nctx, nz), out_shape=jax.ShapeDt...  110 us

profile of v2, /device:TPU:2, one launch (start us, length us, event | category | flops | bytes accessed | tf_op | source)
XLA Modules:
  0.0 112.1 jit_solution(10929592293044817550)
XLA Ops:
  0.0 110.2 %based_layer.1 = bf16[1024,256]{1,0:T(8,128)(2,1)} custom-call(bf16[1024,256]{1,0:T(8,128)(2,1)} %tok.1, s32[8,128]{1,0:T(8,128)} %bitcast.3, bf16[64,4096]{1,0:T(8,128)(2,1)} %bitcast.2, bf16[4096,256]{1,0:T(8,128)(2,1)} %wv_in.1, bf16[4096,512]{1,0:T(8,128)(2,1)} %ww_in.1, bf16[256,4096]{1,0:T(8,128)(2,1)} %wo_in.1, bf16[1536,256]{1,0:T(8,128)(2,1)} %constant.2.clone.table_in), custom_call_target="tpu_custom_call" | custom-call | tf_op jit(solution)/shard_map/based_layer/pallas_call | solution.py:546
  110.2 1.9 %copy.9 = bf16[1024,256]{1,0:T(8,128)(2,1)} copy(bf16[1024,256]{1,0:T(8,128)(2,1)} %based_layer.1) | data formatting | bytes 1048576

commit v3 on v2

--- a/solution.py
+++ b/solution.py
@@ -77,12 +77,13 @@
     out,
     gath, wf, wv, ww, af, av, aw, table,
     feat, wq, kcat, vcat, docc, docr, fq, fk, phiq,
-    docs, lin, win, st_send, st_recv, st_sums, st, mix, wo, sbuf, rbuf,
+    docs, lin, win, st_acc, st_send, st_recv, st_sums, st, mix, wo, sbuf, rbuf,
     load_sem, tok_sem, wo_sem, ring_send, ring_recv, par_send, par_recv,
     wo_send, wo_recv, doc_send, doc_recv, st_ssem, st_rsem, sum_ssem, sum_rsem, tail_send, tail_recv,
     mix_send, mix_recv, rs_send, rs_recv,
 ):
     n_sub = tok.shape[0] // SUB
+    assert n_sub == 4
     units = n_sub * nz
     rows_total = tok.shape[0]
     part = WIDE // nctx
@@ -231,59 +232,6 @@
 
     lax.fori_loop(0, nz, start_wo, 0)
 
-    for load in loads:
-        load.wait()
-
-    lag = 2
-
-    def ring_step(u, carry):
-        @pl.when((u >= n_sub) & (u < units))
-        def _():
-            ring_arrival(u).wait_recv()
-
-            @pl.when(u < units - n_sub)
-            def _():
-                ring_copy(u).start()
-
-            par_copy(u, k, way).start()
-
-        @pl.when(u < units)
-        def _():
-            accumulate(u, k, way)
-
-        @pl.when(u >= lag)
-        def _():
-            par_copy(u - lag, other, -way).wait_recv()
-            accumulate(u - lag, other, -way)
-
-        return carry
-
-    lax.fori_loop(0, units + lag, ring_step, 0)
-
-    def round_rows(i, carry):
-        rows = sub_rows(i)
-        late = pl.ds(pl.multiple_of(LEAD + i * SUB, 128), SUB)
-        feat[rows, :] = af[rows, :].astype(BF16)
-        vcat[late, :] = av[rows, :].astype(BF16)
-        wq[rows, 0:128] = aw[rows, 0:128].astype(BF16)
-        kcat[late, 0:128] = aw[rows, 128:256].astype(BF16)
-        wq[rows, 128:256] = aw[rows, 256:384].astype(BF16)
-        kcat[late, 128:256] = aw[rows, 384:512].astype(BF16)
-        return carry
-
-    lax.fori_loop(0, n_sub, round_rows, 0)
-
-    def tail_copy(n):
-        buf = (kcat, vcat)[n]
-        return pltpu.make_async_remote_copy(
-            src_ref=buf.at[LEAD + rows_total - WIN : LEAD + rows_total],
-            dst_ref=buf.at[LEAD - WIN : LEAD],
-            send_sem=tail_send.at[n],
-            recv_sem=tail_recv.at[n],
-            device_id={"ctx": lax.rem(b + 1, nctx)},
-            device_id_type=MESH,
-        )
-
     mine = doc[...].astype(F32)
     last_doc = mine[7:8, 127:128]
     for i in range(8):
@@ -291,15 +239,100 @@
         docr[0:1, LEAD + i * 128 : LEAD + (i + 1) * 128] = row
         docc[i * 128 : (i + 1) * 128, :] = jnp.broadcast_to(row, (128, 128)).T
 
+    st_acc[...] = jnp.zeros_like(st_acc)
+    for load in loads:
+        load.wait()
+
+    lag = 6
+
+    def own_unit(u):
+        @pl.when(u >= n_sub)
+        def _():
+            ring_arrival(u).wait_recv()
+
+            @pl.when(u < units - n_sub)
+            def _():
+                ring_copy(u).start()
+
+            par_copy(u, k, way).start()
+
+        accumulate(u, k, way)
+
+    def partner_unit(u):
+        par_copy(u, other, -way).wait_recv()
+        accumulate(u, other, -way)
+
+    def ring_step(u, carry):
+        own_unit(u)
+
+        @pl.when(u >= lag)
+        def _():
+            partner_unit(u - lag)
+
+        return carry
+
+    turn = units - n_sub
+    lax.fori_loop(0, turn, ring_step, 0)
+
     one_k, two_k = factor_bias((WIDE, 1), 0)
-    keeps = docr[0:1, LEAD : LEAD + rows_total] == last_doc
+
+    def finish(i):
+        rows = sub_rows(i)
+        late = pl.ds(pl.multiple_of(LEAD + i * SUB, 128), SUB)
+        x = af[rows, :].astype(BF16)
+        v = av[rows, :].astype(BF16)
+        feat[rows, :] = x
+        vcat[late, :] = v
+        keeps = docr[0:1, late] == last_doc
+        for j in range(2):
+            at = 256 + 512 * j
+            left = dot_nt(table[at : at + 256, 0:64], x) + one_k
+            right = dot_nt(table[at + 256 : at + 512, 0:64], x) + two_k
+            phi_k = jnp.where(keeps, left * right, 0.0).astype(BF16)
+            st_acc[j] += dot(phi_k, v[:, j * 128 : (j + 1) * 128])
+        wq[rows, 0:128] = aw[rows, 0:128].astype(BF16)
+        kcat[late, 0:128] = aw[rows, 128:256].astype(BF16)
+        wq[rows, 128:256] = aw[rows, 256:384].astype(BF16)
+        kcat[late, 128:256] = aw[rows, 384:512].astype(BF16)
+
+    def catch_up(n, carry):
+        own_unit(turn + n)
+
+        def partner_next(m, inner):
+            partner_unit(turn - lag + 3 * n + m)
+            return inner
+
+        lax.fori_loop(0, 3, partner_next, 0)
+        return carry
+
+    def finish_early(n, carry):
+        own_unit(turn + 2 + n)
+        partner_unit(turn + n)
+        finish(n)
+        return carry
+
+    def finish_late(n, carry):
+        partner_unit(turn + 2 + n)
+        finish(2 + n)
+        return carry
+
+    lax.fori_loop(0, 2, catch_up, 0)
+    lax.fori_loop(0, 2, finish_early, 0)
+    lax.fori_loop(0, 2, finish_late, 0)
+
+    def tail_copy(n):
+        buf = (kcat, vcat)[n]
+        return pltpu.make_async_remote_copy(
+            src_ref=buf.at[LEAD + rows_total - WIN : LEAD + rows_total],
+            dst_ref=buf.at[LEAD - WIN : LEAD],
+            send_sem=tail_send.at[n],
+            recv_sem=tail_recv.at[n],
+            device_id={"ctx": lax.rem(b + 1, nctx)},
+            device_id_type=MESH,
+        )
+
     for j in range(2):
-        at = 256 + 512 * j
-        left = dot_nt(table[at : at + 256, 0:64], feat[...]) + one_k
-        right = dot_nt(table[at + 256 : at + 512, 0:64], feat[...]) + two_k
-        phi_k = jnp.where(keeps, left * right, 0.0).astype(BF16)
-        local = dot(phi_k, vcat[LEAD : LEAD + rows_total, j * 128 : (j + 1) * 128])
-        st_send[:, j * part : (j + 1) * part, :] = local.astype(BF16).reshape(nctx, part, 128)
+        st_send[:, j * part : (j + 1) * part, :] = st_acc[j].astype(BF16).reshape(nctx, part, 128)
 
     def st_copy(c, slot):
         return pltpu.make_async_remote_copy(
@@ -365,21 +398,22 @@
     docs[b] = doc[...]
     st_recv[b] = st_send[b]
 
-    def add_block(c, carry):
-        sums, sums_doc = carry
-        block_doc = docs[c][7:8, 127:128]
-        sums = st_recv[c].astype(F32) + jnp.where(sums_doc == block_doc, sums, 0.0)
+    sums = jnp.zeros((2 * part, 128), F32)
+    for c in range(nctx - 1):
+        same = docs[c][7:8, 127:128] == docs[max(c - 1, 0)][7:8, 127:128]
+        sums = st_recv[c].astype(F32) + jnp.where(same, sums, 0.0)
         st_sums[c + 1] = sums.astype(BF16)
 
-        @pl.when(c + 1 != b)
-        def _():
-            sum_back(c + 1, b).start()
-
-        return sums, block_doc
-
-    lax.fori_loop(
-        0, nctx - 1, add_block, (jnp.zeros((2 * part, 128), F32), jnp.full((1, 1), -1, jnp.int32))
-    )
+    def start_sum(n, carry):
+        c = lax.rem(b + n, nctx)
+
+        @pl.when(c > 0)
+        def _():
+            sum_back(c, b).start()
+
+        return carry
+
+    lax.fori_loop(1, nctx, start_sum, 0)
 
     @pl.when(b == 0)
     def _():
@@ -569,6 +603,7 @@
                 vmem((nctx, 8, 128), jnp.int32),
                 vmem((rows, 256), F32),
                 vmem((rows, 256), F32),
+                vmem((2, WIDE, 128), F32),
                 vmem((nctx, 2 * WIDE // nctx, 128), BF16),
                 vmem((nctx, 2 * WIDE // nctx, 128), BF16),
                 vmem((nctx, 2 * WIDE // nctx, 128), BF16),
@@ -600,7 +635,7 @@
                 dma((units,)),
             ],
             compiler_params=pltpu.CompilerParams(
-                collective_id=0, has_side_effects=True, vmem_limit_bytes=67043328 - 600 * 1024
+                collective_id=0, has_side_effects=True, vmem_limit_bytes=67043328 - 11000 * 1024
             ),
             name="based_layer",
         )(

time: 113 us -> 110 us (0.973)
  Pallas kernels: 110 us -> 108 us
    pallas_call x1, Pallas kernels: 110 us -> 108 us  [shards(): pl.pallas_call(functools.partial(kernel, nctx, nz), out_shape=jax.ShapeDt...]
where the time goes in v3:
time: 110 us
  Pallas kernels  108 us (98%)
  local copies, waits for them, and re-layouts  1.48 us (1%)
    pallas_call x1, Pallas kernels, shards(): pl.pallas_call(functools.partial(kernel, nctx, nz), out_shape=jax.ShapeDt...  108 us

profile of v3, /device:TPU:2, one launch (start us, length us, event | category | flops | bytes accessed | tf_op | source)
XLA Modules:
  0.0 110.0 jit_solution(4558587030739550408)
XLA Ops:
  0.0 0.0 copy-start
  0.0 0.7 copy-done
  0.7 108.5 %based_layer.1 = bf16[1024,256]{1,0:T(8,128)(2,1)S(1)} custom-call(bf16[1024,256]{1,0:T(8,128)(2,1)} %tok.1, s32[8,128]{1,0:T(8,128)S(1)} %bitcast.2, bf16[64,4096]{1,0:T(8,128)(2,1)} %bitcast.3, bf16[4096,256]{1,0:T(8,128)(2,1)} %wv_in.1, bf16[4096,512]{1,0:T(8,128)(2,1)} %ww_in.1, bf16[256,4096]{1,0:T(8,128)(2,1)} %wo_in.1, ...), custom_call_target="tpu_custom_call" | custom-call | tf_op jit(solution)/shard_map/based_layer/pallas_call | solution.py:580
  109.2 0.8 copy.9
Async XLA Ops:
  0.0 0.7 copy-start

commit v4 on v3

--- a/solution.py
+++ b/solution.py
@@ -73,9 +73,9 @@
 
 def kernel(
     nctx, nz,
-    tok, doc, wf_in, wv_in, ww_in, wo_in, table_in,
+    tok, doc_in, wf_in, wv_in, ww_in, wo_in, table_in,
     out,
-    gath, wf, wv, ww, af, av, aw, table,
+    doc, gath, wf, wv, ww, af, av, aw, table,
     feat, wq, kcat, vcat, docc, docr, fq, fk, phiq,
     docs, lin, win, st_acc, st_send, st_recv, st_sums, st, mix, wo, sbuf, rbuf,
     load_sem, tok_sem, wo_sem, ring_send, ring_recv, par_send, par_recv,
@@ -97,11 +97,25 @@
     behind = lax.rem(z - way + nz, nz) * 2 + k
     partner = z * 2 + other
 
+    far_first = sorted(range(1, nctx), key=lambda n: -min(n // 4, 4 - n // 4) - min(n % 4, 4 - n % 4))
+
     def sub_rows(i):
         return pl.ds(pl.multiple_of(i * SUB, SUB), SUB)
 
     def cols(block):
         return pl.ds(pl.multiple_of(block * 256, 256), 256)
+
+    barrier = pltpu.get_barrier_semaphore()
+
+    def greet(n, carry):
+        pl.semaphore_signal(
+            barrier, inc=1, device_id={"ctx": lax.rem(b + 1 + n, nctx)}, device_id_type=MESH
+        )
+        return carry
+
+    for peer in (ahead, behind, partner):
+        pl.semaphore_signal(barrier, inc=1, device_id={"head": peer}, device_id_type=MESH)
+    lax.fori_loop(0, nctx - 1, greet, 0)
 
     def bulk(ref, sem):
         return pltpu.make_async_copy(ref, ref, sem.at[0])
@@ -109,7 +123,7 @@
     loads = [
         pltpu.make_async_copy(src, dst, load_sem.at[n])
         for n, (src, dst) in enumerate(
-            [(wf_in, wf), (wv_in, wv), (ww_in, ww), (table_in, table)]
+            [(doc_in, doc), (wf_in, wf), (wv_in, wv), (ww_in, ww), (table_in, table)]
         )
     ]
 
@@ -121,23 +135,19 @@
     for load in loads:
         load.start()
 
-    kcat[0:LEAD, :] = jnp.zeros((LEAD, 256), BF16)
-    vcat[0:LEAD, :] = jnp.zeros((LEAD, 256), BF16)
-
-    barrier = pltpu.get_barrier_semaphore()
-
-    def greet(n, carry):
-        pl.semaphore_signal(
-            barrier, inc=1, device_id={"ctx": lax.rem(b + 1 + n, nctx)}, device_id_type=MESH
-        )
-        return carry
-
-    for peer in (ahead, behind, partner):
-        pl.semaphore_signal(barrier, inc=1, device_id={"head": peer}, device_id_type=MESH)
-    lax.fori_loop(0, nctx - 1, greet, 0)
     af[...] = jnp.zeros_like(af)
     av[...] = jnp.zeros_like(av)
     aw[...] = jnp.zeros_like(aw)
+    st_acc[...] = jnp.zeros_like(st_acc)
+    no_rows = jnp.zeros((LEAD - WIN, 256), BF16)
+    for buf in (kcat, vcat):
+        buf[0 : LEAD - WIN, :] = no_rows
+
+    @pl.when(b == 0)
+    def _():
+        for buf in (kcat, vcat):
+            buf[LEAD - WIN : LEAD, :] = no_rows
+
     pl.semaphore_wait(barrier, nctx + 2)
 
     def ring_copy(u):
@@ -181,20 +191,24 @@
             device_id_type=MESH,
         )
 
-    def accumulate(u, side, turn):
+    def accumulate(u, side, turn, what="both"):
         s = u // n_sub
         rows = sub_rows(u - s * n_sub)
         src = lax.rem(z - s * turn + 2 * nz, nz)
         x = gath[side, src, rows, :]
         w_rows = cols(src * 2 + side)
-        af[rows, :] += dot_nt(x, wf[:, w_rows])
-        av[rows, :] += dot(x, wv[w_rows, :])
-        aw[rows, :] += dot(x, ww[w_rows, :])
+        if what != "window":
+            af[rows, :] += dot_nt(x, wf[:, w_rows])
+            av[rows, :] += dot(x, wv[w_rows, :])
+        if what != "state":
+            aw[rows, :] += dot(x, ww[w_rows, :])
 
     for i in range(n_sub):
         tok_load(i).wait()
         ring_copy(i).start()
         par_copy(i, k, way).start()
+
+    loads[0].wait()
 
     def doc_copy(c, slot):
         return pltpu.make_async_remote_copy(
@@ -239,8 +253,7 @@
         docr[0:1, LEAD + i * 128 : LEAD + (i + 1) * 128] = row
         docc[i * 128 : (i + 1) * 128, :] = jnp.broadcast_to(row, (128, 128)).T
 
-    st_acc[...] = jnp.zeros_like(st_acc)
-    for load in loads:
+    for load in loads[1:]:
         load.wait()
 
     lag = 6
@@ -258,9 +271,9 @@
 
         accumulate(u, k, way)
 
-    def partner_unit(u):
+    def partner_unit(u, what="both"):
         par_copy(u, other, -way).wait_recv()
-        accumulate(u, other, -way)
+        accumulate(u, other, -way, what)
 
     def ring_step(u, carry):
         own_unit(u)
@@ -290,10 +303,6 @@
             right = dot_nt(table[at + 256 : at + 512, 0:64], x) + two_k
             phi_k = jnp.where(keeps, left * right, 0.0).astype(BF16)
             st_acc[j] += dot(phi_k, v[:, j * 128 : (j + 1) * 128])
-        wq[rows, 0:128] = aw[rows, 0:128].astype(BF16)
-        kcat[late, 0:128] = aw[rows, 128:256].astype(BF16)
-        wq[rows, 128:256] = aw[rows, 256:384].astype(BF16)
-        kcat[late, 128:256] = aw[rows, 384:512].astype(BF16)
 
     def catch_up(n, carry):
         own_unit(turn + n)
@@ -312,7 +321,7 @@
         return carry
 
     def finish_late(n, carry):
-        partner_unit(turn + 2 + n)
+        partner_unit(turn + 2 + n, "state")
         finish(2 + n)
         return carry
 
@@ -344,11 +353,24 @@
             device_id_type=MESH,
         )
 
-    def start_state(n, carry):
+    for n in far_first:
         st_copy(lax.rem(b + n, nctx), b).start()
-        return carry
-
-    lax.fori_loop(1, nctx, start_state, 0)
+
+    def window_rows(i, carry):
+        rows = sub_rows(i)
+        late = pl.ds(pl.multiple_of(LEAD + i * SUB, 128), SUB)
+        wq[rows, 0:128] = aw[rows, 0:128].astype(BF16)
+        kcat[late, 0:128] = aw[rows, 128:256].astype(BF16)
+        wq[rows, 128:256] = aw[rows, 256:384].astype(BF16)
+        kcat[late, 128:256] = aw[rows, 384:512].astype(BF16)
+        return carry
+
+    def window_late(n, carry):
+        accumulate(turn + 2 + n, other, -way, "window")
+        return carry
+
+    lax.fori_loop(0, 2, window_late, 0)
+    lax.fori_loop(0, n_sub, window_rows, 0)
 
     @pl.when(b < nctx - 1)
     def _():
@@ -404,16 +426,13 @@
         sums = st_recv[c].astype(F32) + jnp.where(same, sums, 0.0)
         st_sums[c + 1] = sums.astype(BF16)
 
-    def start_sum(n, carry):
-        c = lax.rem(b + n, nctx)
-
+    def start_sum(c):
         @pl.when(c > 0)
         def _():
             sum_back(c, b).start()
 
-        return carry
-
-    lax.fori_loop(1, nctx, start_sum, 0)
+    for n in far_first:
+        start_sum(lax.rem(b + n, nctx))
 
     @pl.when(b == 0)
     def _():
@@ -425,21 +444,20 @@
         tail_copy(1).wait_recv()
         docr[0:1, 0:LEAD] = docs[b - 1][7:8, :].astype(F32)
 
-    reach = LEAD + SUB
-    gap = lax.broadcasted_iota(jnp.int32, (SUB, reach), 1) - lax.broadcasted_iota(
-        jnp.int32, (SUB, reach), 0
+    tile, reach = 128, LEAD + 128
+    gap = lax.broadcasted_iota(jnp.int32, (tile, reach), 1) - lax.broadcasted_iota(
+        jnp.int32, (tile, reach), 0
     )
     band = (gap > LEAD - WIN) & (gap <= LEAD)
-    for i in range(n_sub):
-        lo, hi = i * SUB, (i + 1) * SUB
+    for i in range(rows_total // tile):
+        lo, hi = i * tile, (i + 1) * tile
         within = band & (docc[lo:hi, 0:1] == docr[0:1, lo : lo + reach])
         for j in range(2):
             at = slice(j * 128, (j + 1) * 128)
-            logits = dot_nt(wq[lo:hi, at], kcat[lo : lo + reach, at]) * HEAD_DIM ** (-0.5)
-            logits = jnp.where(within, logits, -1e30)
+            logits = jnp.where(within, dot_nt(wq[lo:hi, at], kcat[lo : lo + reach, at]), -1e30)
             top = jnp.max(logits, -1, keepdims=True)
-            weights = jnp.where(within, jnp.exp(logits - top), 0.0)
-            probs = (weights / jnp.sum(weights, -1, keepdims=True)).astype(BF16)
+            weights = jnp.exp((logits - top) * HEAD_DIM ** (-0.5))
+            probs = (weights * (1.0 / jnp.sum(weights, -1, keepdims=True))).astype(BF16)
             win[lo:hi, at] = dot(probs, vcat[lo : lo + reach, at])
 
     @pl.when(b == 0)
@@ -580,9 +598,10 @@
         return pl.pallas_call(
             functools.partial(kernel, nctx, nz),
             out_shape=jax.ShapeDtypeStruct((rows, 256), BF16),
-            in_specs=[hbm_space, vmem_space] + [hbm_space] * 5,
+            in_specs=[hbm_space] * 7,
             out_specs=vmem_space,
             scratch_shapes=[
+                vmem((8, 128), jnp.int32),
                 vmem((2, nz, rows, 256), BF16),
                 vmem((64, width), BF16),
                 vmem((width, 256), BF16),
@@ -612,7 +631,7 @@
                 vmem((2, nz, 256, 256), BF16),
                 vmem((nz - 1, n_sub, SUB, 256), BF16),
                 vmem((nz - 1, n_sub, SUB, 256), BF16),
-                dma((4,)),
+                dma((5,)),
                 dma((n_sub,)),
                 dma((1,)),
                 dma((1,)),
@@ -632,7 +651,7 @@
                 dma((1,)),
                 dma((n_sub,)),
                 dma((1,)),
-                dma((units,)),
+                dma((units - n_sub,)),
             ],
             compiler_params=pltpu.CompilerParams(
                 collective_id=0, has_side_effects=True, vmem_limit_bytes=67043328 - 11000 * 1024
@@ -640,7 +659,7 @@
             name="based_layer",
         )(
             tokens,
-            doc_ids.reshape(8, 128),
+            pltpu.with_memory_space_constraint(doc_ids.reshape(8, 128), pltpu.HBM),
             w_feat.T,
             w_value,
             w_window,

time: 110 us -> 109 us (level)
  no operation moved by 1% of the time
where the time goes in v4:
time: 109 us
  Pallas kernels  108 us (99%)
    pallas_call x1, Pallas kernels, shards(): pl.pallas_call(functools.partial(kernel, nctx, nz), out_shape=jax.ShapeDt...  108 us

profile of v4, /device:TPU:2, one launch (start us, length us, event | category | flops | bytes accessed | tf_op | source)
XLA Modules:
  0.0 108.8 jit_solution(2807742432577005709)
XLA Ops:
  0.0 108.0 %based_layer.1 = bf16[1024,256]{1,0:T(8,128)(2,1)S(1)} custom-call(bf16[1024,256]{1,0:T(8,128)(2,1)} %tok.1, s32[8,128]{1,0:T(8,128)} %bitcast.3, bf16[64,4096]{1,0:T(8,128)(2,1)} %bitcast.2, bf16[4096,256]{1,0:T(8,128)(2,1)} %wv_in.1, bf16[4096,512]{1,0:T(8,128)(2,1)} %ww_in.1, bf16[256,4096]{1,0:T(8,128)(2,1)} %wo_in.1, ...), custom_call_target="tpu_custom_call" | custom-call | tf_op jit(solution)/shard_map/based_layer/pallas_call | solution.py:598
  108.0 0.8 copy.9

commit v5 on v4

--- a/solution.py
+++ b/solution.py
@@ -14,7 +14,7 @@
 SUB = 256
 WIDE = 256
 PART = 32
-TABLE = 1536
+TABLE = 1408
 LEAD = 128
 F32 = jnp.float32
 BF16 = jnp.bfloat16
@@ -40,19 +40,18 @@
             weight[p + 1 + n] = 0.25
     query = np.zeros((2, 2, 4 * FEAT, WIDE), np.float32)
     key = np.zeros((2, 2, WIDE, 4 * FEAT), np.float32)
-    pick = np.zeros((2, 2, 4 * FEAT, 128), np.float32)
+    pick = np.zeros((2, 4 * FEAT, 4 * FEAT), np.float32)
     for head in range(2):
         at = head * 2 * FEAT
         query[head, 0, at : at + FEAT] = first * weight
         query[head, 1, at : at + FEAT] = second
         key[head, 0, :, at + FEAT : at + 2 * FEAT] = first.T
         key[head, 1, :, at + FEAT : at + 2 * FEAT] = second.T
-        pick[head, 0, at : at + FEAT, :FEAT] = np.eye(FEAT)
-        pick[head, 1, at + FEAT : at + 2 * FEAT, :FEAT] = np.eye(FEAT)
+        pick[head, at : at + FEAT, at + FEAT : at + 2 * FEAT] = np.eye(FEAT)
     table = np.zeros((TABLE, WIDE), np.float32)
     table[0:256] = query.reshape(256, WIDE)
     table[256:1280, 0 : 4 * FEAT] = key.reshape(4 * WIDE, 4 * FEAT)
-    table[1280:1536, 0:128] = pick.reshape(256, 128)
+    table[1280:1408, 0 : 4 * FEAT] = pick.reshape(128, 4 * FEAT)
     return jnp.asarray(table, BF16)
 
 
@@ -76,11 +75,11 @@
     tok, doc_in, wf_in, wv_in, ww_in, wo_in, table_in,
     out,
     doc, gath, wf, wv, ww, af, av, aw, table,
-    feat, wq, kcat, vcat, docc, docr, fq, fk, phiq,
+    feat, wq, kcat, vcat, docc, docr, fq, phiq,
     docs, lin, win, st_acc, st_send, st_recv, st_sums, st, mix, wo, sbuf, rbuf,
     load_sem, tok_sem, wo_sem, ring_send, ring_recv, par_send, par_recv,
     wo_send, wo_recv, doc_send, doc_recv, st_ssem, st_rsem, sum_ssem, sum_rsem, tail_send, tail_recv,
-    mix_send, mix_recv, rs_send, rs_recv,
+    mix_send, mix_recv, rs_send, rs_recv, told,
 ):
     n_sub = tok.shape[0] // SUB
     assert n_sub == 4
@@ -105,17 +104,25 @@
     def cols(block):
         return pl.ds(pl.multiple_of(block * 256, 256), 256)
 
+    side = 4 if nctx > 4 else nctx
+    base = b // side * side
+    turns = [1] if side == 2 else [1, side - 1]
+    beside = [base + lax.rem(b - base + n, side) for n in turns]
+    if nctx > side:
+        turns = [side] if nctx == 2 * side else [side, nctx - side]
+        beside += [lax.rem(b + n, nctx) for n in turns]
     barrier = pltpu.get_barrier_semaphore()
-
-    def greet(n, carry):
-        pl.semaphore_signal(
-            barrier, inc=1, device_id={"ctx": lax.rem(b + 1 + n, nctx)}, device_id_type=MESH
-        )
-        return carry
-
     for peer in (ahead, behind, partner):
         pl.semaphore_signal(barrier, inc=1, device_id={"head": peer}, device_id_type=MESH)
-    lax.fori_loop(0, nctx - 1, greet, 0)
+    for peer in beside:
+        pl.semaphore_signal(barrier, inc=1, device_id={"ctx": peer}, device_id_type=MESH)
+
+    def tell(n):
+        for peer in beside:
+            pl.semaphore_signal(told.at[n], inc=1, device_id={"ctx": peer}, device_id_type=MESH)
+
+    def hear(n):
+        pl.semaphore_wait(told.at[n], len(beside))
 
     def bulk(ref, sem):
         return pltpu.make_async_copy(ref, ref, sem.at[0])
@@ -148,7 +155,7 @@
         for buf in (kcat, vcat):
             buf[LEAD - WIN : LEAD, :] = no_rows
 
-    pl.semaphore_wait(barrier, nctx + 2)
+    pl.semaphore_wait(barrier, len(beside) + 3)
 
     def ring_copy(u):
         s = u // n_sub
@@ -207,6 +214,7 @@
         tok_load(i).wait()
         ring_copy(i).start()
         par_copy(i, k, way).start()
+    tell(0)
 
     loads[0].wait()
 
@@ -233,11 +241,6 @@
     def wo_load(d):
         return pltpu.make_async_copy(wo_in.at[:, cols(d * 2 + k)], wo.at[k, d], wo_sem.at[0])
 
-    def start_doc(n, carry):
-        doc_copy(lax.rem(b + n, nctx), b).start()
-        return carry
-
-    lax.fori_loop(1, nctx, start_doc, 0)
 
     def start_wo(d, carry):
         wo_copy(d, k, other).start()
@@ -258,7 +261,7 @@
 
     lag = 6
 
-    def own_unit(u):
+    def own_unit(u, what="both"):
         @pl.when(u >= n_sub)
         def _():
             ring_arrival(u).wait_recv()
@@ -269,7 +272,7 @@
 
             par_copy(u, k, way).start()
 
-        accumulate(u, k, way)
+        accumulate(u, k, way, what)
 
     def partner_unit(u, what="both"):
         par_copy(u, other, -way).wait_recv()
@@ -285,7 +288,20 @@
         return carry
 
     turn = units - n_sub
-    lax.fori_loop(0, turn, ring_step, 0)
+    lax.fori_loop(0, 2 * n_sub, ring_step, 0)
+    hear(0)
+    tell(1)
+    lax.fori_loop(2 * n_sub, 3 * n_sub, ring_step, 0)
+    hear(1)
+    tell(2)
+    lax.fori_loop(3 * n_sub, turn, ring_step, 0)
+    hear(2)
+
+    def start_doc(n, carry):
+        doc_copy(lax.rem(b + n, nctx), b).start()
+        return carry
+
+    lax.fori_loop(1, nctx, start_doc, 0)
 
     one_k, two_k = factor_bias((WIDE, 1), 0)
 
@@ -315,8 +331,8 @@
         return carry
 
     def finish_early(n, carry):
-        own_unit(turn + 2 + n)
-        partner_unit(turn + n)
+        own_unit(turn + 2 + n, "state")
+        partner_unit(turn + n, "state")
         finish(n)
         return carry
 
@@ -366,6 +382,8 @@
         return carry
 
     def window_late(n, carry):
+        accumulate(turn + 2 + n, k, way, "window")
+        accumulate(turn + n, other, -way, "window")
         accumulate(turn + 2 + n, other, -way, "window")
         return carry
 
@@ -376,6 +394,60 @@
     def _():
         tail_copy(0).start()
         tail_copy(1).start()
+
+    def feature_rows(i, carry):
+        rows = sub_rows(i)
+        x = feat[rows, :]
+        for j in range(2):
+            at = 1280 + 64 * j
+            fq[j, rows, :] = dot(x, table[at : at + 64, 0:64]).astype(BF16)
+        return carry
+
+    lax.fori_loop(0, n_sub, feature_rows, 0)
+
+    def taylor_rows(i):
+        lo, hi = i * SUB, (i + 1) * SUB
+        t_pos = lax.broadcasted_iota(jnp.int32, (SUB, hi), 0) + lo
+        s_pos = lax.broadcasted_iota(jnp.int32, (SUB, hi), 1)
+        allowed = (s_pos <= t_pos) & (docc[lo:hi, 0:1] == docr[0:1, LEAD : LEAD + hi])
+        for j in range(2):
+            d = dot_nt(fq[j, lo:hi, :], feat[0:hi, :])
+            taylor = jnp.where(allowed, 1.0 + d * (0.25 + d * 0.03125), 0.0).astype(BF16)
+            lin[lo:hi, j * 128 : (j + 1) * 128] = dot(
+                taylor, vcat[LEAD : LEAD + hi, j * 128 : (j + 1) * 128]
+            )
+
+    taylor_rows(0)
+    taylor_rows(1)
+
+    def sum_back(c, slot):
+        return pltpu.make_async_remote_copy(
+            src_ref=st_sums.at[c],
+            dst_ref=st.at[slot],
+            send_sem=sum_ssem.at[0],
+            recv_sem=sum_rsem.at[0],
+            device_id={"ctx": c},
+            device_id_type=MESH,
+        )
+
+    bulk(docs.at[0 : nctx - 1], doc_recv).wait()
+    bulk(st_recv.at[0 : nctx - 1], st_rsem).wait()
+    docs[b] = doc[...]
+    st_recv[b] = st_send[b]
+
+    sums = jnp.zeros((2 * part, 128), F32)
+    for c in range(nctx - 1):
+        same = docs[c][7:8, 127:128] == docs[max(c - 1, 0)][7:8, 127:128]
+        sums = st_recv[c].astype(F32) + jnp.where(same, sums, 0.0)
+        st_sums[c + 1] = sums.astype(BF16)
+
+    def start_sum(c):
+        @pl.when(c > 0)
+        def _():
+            sum_back(c, b).start()
+
+    for n in far_first:
+        start_sum(lax.rem(b + n, nctx))
 
     one_q, two_q = factor_bias((1, WIDE), 1)
 
@@ -386,53 +458,10 @@
             left = dot(x, table[128 * j : 128 * j + 64, :]) + one_q
             right = dot(x, table[128 * j + 64 : 128 * j + 128, :]) + two_q
             phiq[j, rows, :] = (left * right).astype(BF16)
-            at = 1280 + 128 * j
-            fq[j, rows, :] = dot(x, table[at : at + 64, 0:128]).astype(BF16)
-            fk[j, rows, :] = dot(x, table[at + 64 : at + 128, 0:128]).astype(BF16)
         return carry
 
     lax.fori_loop(0, n_sub, query_rows, 0)
-
-    for i in range(n_sub):
-        lo, hi = i * SUB, (i + 1) * SUB
-        t_pos = lax.broadcasted_iota(jnp.int32, (SUB, hi), 0) + lo
-        s_pos = lax.broadcasted_iota(jnp.int32, (SUB, hi), 1)
-        allowed = (s_pos <= t_pos) & (docc[lo:hi, 0:1] == docr[0:1, LEAD : LEAD + hi])
-        for j in range(2):
-            d = dot_nt(fq[j, lo:hi, :], fk[j, 0:hi, :])
-            taylor = jnp.where(allowed, 1.0 + d * (0.25 + d * 0.03125), 0.0).astype(BF16)
-            lin[lo:hi, j * 128 : (j + 1) * 128] = dot(
-                taylor, vcat[LEAD : LEAD + hi, j * 128 : (j + 1) * 128]
-            )
-
-    def sum_back(c, slot):
-        return pltpu.make_async_remote_copy(
-            src_ref=st_sums.at[c],
-            dst_ref=st.at[slot],
-            send_sem=sum_ssem.at[0],
-            recv_sem=sum_rsem.at[0],
-            device_id={"ctx": c},
-            device_id_type=MESH,
-        )
-
-    bulk(docs.at[0 : nctx - 1], doc_recv).wait()
-    bulk(st_recv.at[0 : nctx - 1], st_rsem).wait()
-    docs[b] = doc[...]
-    st_recv[b] = st_send[b]
-
-    sums = jnp.zeros((2 * part, 128), F32)
-    for c in range(nctx - 1):
-        same = docs[c][7:8, 127:128] == docs[max(c - 1, 0)][7:8, 127:128]
-        sums = st_recv[c].astype(F32) + jnp.where(same, sums, 0.0)
-        st_sums[c + 1] = sums.astype(BF16)
-
-    def start_sum(c):
-        @pl.when(c > 0)
-        def _():
-            sum_back(c, b).start()
-
-    for n in far_first:
-        start_sum(lax.rem(b + n, nctx))
+    taylor_rows(2)
 
     @pl.when(b == 0)
     def _():
@@ -547,6 +576,10 @@
         return carry
 
     def first_step(i, carry):
+        @pl.when(i == n_sub - 1)
+        def _():
+            taylor_rows(n_sub - 1)
+
         @pl.when(i < n_sub)
         def _():
             mix_rows(i, 0)
@@ -616,8 +649,7 @@
                 vmem((LEAD + rows, 256), BF16),
                 vmem((rows, 128), F32),
                 vmem((1, LEAD + rows), F32),
-                vmem((2, rows, 128), BF16),
-                vmem((2, rows, 128), BF16),
+                vmem((2, rows, 64), BF16),
                 vmem((2, rows, WIDE), BF16),
                 vmem((nctx, 8, 128), jnp.int32),
                 vmem((rows, 256), F32),
@@ -652,6 +684,7 @@
                 dma((n_sub,)),
                 dma((1,)),
                 dma((units - n_sub,)),
+                pltpu.SemaphoreType.REGULAR((3,)),
             ],
             compiler_params=pltpu.CompilerParams(
                 collective_id=0, has_side_effects=True, vmem_limit_bytes=67043328 - 11000 * 1024

time: 109 us -> 107 us (0.982)
  Pallas kernels: 108 us -> 106 us
    pallas_call x1, Pallas kernels: 108 us -> 106 us  [shards(): pl.pallas_call(functools.partial(kernel, nctx, nz), out_shape=jax.ShapeDt...]
where the time goes in v5:
time: 107 us
  Pallas kernels  106 us (99%)
    pallas_call x1, Pallas kernels, shards(): pl.pallas_call(functools.partial(kernel, nctx, nz), out_shape=jax.ShapeDt...  106 us

profile of v5, /device:TPU:2, one launch (start us, length us, event | category | flops | bytes accessed | tf_op | source)
XLA Modules:
  0.0 106.8 jit_solution(16110464024482853700)
XLA Ops:
  0.0 106.0 %based_layer.1 = bf16[1024,256]{1,0:T(8,128)(2,1)S(1)} custom-call(bf16[1024,256]{1,0:T(8,128)(2,1)} %tok.1, s32[8,128]{1,0:T(8,128)} %bitcast.3, bf16[64,4096]{1,0:T(8,128)(2,1)} %bitcast.2, bf16[4096,256]{1,0:T(8,128)(2,1)} %wv_in.1, bf16[4096,512]{1,0:T(8,128)(2,1)} %ww_in.1, bf16[256,4096]{1,0:T(8,128)(2,1)} %wo_in.1, ...), custom_call_target="tpu_custom_call" | custom-call | tf_op jit(solution)/shard_map/based_layer/pallas_call | solution.py:631
  106.0 0.8 copy.9

commit v6 on v5

--- a/solution.py
+++ b/solution.py
@@ -13,8 +13,8 @@
 WIN = 64
 SUB = 256
 WIDE = 256
-PART = 32
-TABLE = 1408
+PACKED = 160
+TABLE = 1024
 LEAD = 128
 F32 = jnp.float32
 BF16 = jnp.bfloat16
@@ -25,33 +25,28 @@
     first = np.zeros((FEAT, WIDE), np.float32)
     second = np.zeros((FEAT, WIDE), np.float32)
     weight = np.zeros((WIDE,), np.float32)
-    for g in range(8):
-        for r in range(FEAT):
-            p = g * PART + r
-            first[r, p] = 1.0
-            second[(r + g) % FEAT, p] = 1.0
-            weight[p] = 1.0 / 32 if g == 0 else 2.0 / 32
-        p = g * PART + 16
-        first[g, p] = 1.0
-        second[g + 8, p] = 1.0
-        weight[p] = 2.0 / 32
-        for n in range(2):
-            first[2 * g + n, p + 1 + n] = 1.0
-            weight[p + 1 + n] = 0.25
+    for p in range(136):
+        i, gap = p % FEAT, p // FEAT
+        first[i, p] = 1.0
+        second[(i + gap) % FEAT, p] = 1.0
+        weight[p] = 1.0 / 32 if gap == 0 else 2.0 / 32
+    for i in range(FEAT):
+        first[i, 144 + i] = 1.0
+        weight[144 + i] = 0.25
     query = np.zeros((2, 2, 4 * FEAT, WIDE), np.float32)
-    key = np.zeros((2, 2, WIDE, 4 * FEAT), np.float32)
+    key = np.zeros((2, 2, PACKED, 4 * FEAT), np.float32)
     pick = np.zeros((2, 4 * FEAT, 4 * FEAT), np.float32)
     for head in range(2):
         at = head * 2 * FEAT
         query[head, 0, at : at + FEAT] = first * weight
         query[head, 1, at : at + FEAT] = second
-        key[head, 0, :, at + FEAT : at + 2 * FEAT] = first.T
-        key[head, 1, :, at + FEAT : at + 2 * FEAT] = second.T
+        key[head, 0, :, at + FEAT : at + 2 * FEAT] = first.T[:PACKED]
+        key[head, 1, :, at + FEAT : at + 2 * FEAT] = second.T[:PACKED]
         pick[head, at : at + FEAT, at + FEAT : at + 2 * FEAT] = np.eye(FEAT)
     table = np.zeros((TABLE, WIDE), np.float32)
     table[0:256] = query.reshape(256, WIDE)
-    table[256:1280, 0 : 4 * FEAT] = key.reshape(4 * WIDE, 4 * FEAT)
-    table[1280:1408, 0 : 4 * FEAT] = pick.reshape(128, 4 * FEAT)
+    table[256:896, 0 : 4 * FEAT] = key.reshape(4 * PACKED, 4 * FEAT)
+    table[896:1024, 0 : 4 * FEAT] = pick.reshape(128, 4 * FEAT)
     return jnp.asarray(table, BF16)
 
 
@@ -65,8 +60,8 @@
 
 def factor_bias(shape, dim):
     p = lax.broadcasted_iota(jnp.int32, shape, dim)
-    one = jnp.where(p == 19, 1.0, 0.0)
-    two = jnp.where((p == 19) | (p % PART == 17) | (p % PART == 18), 1.0, 0.0)
+    one = jnp.where(p == 136, 1.0, 0.0)
+    two = jnp.where((p == 136) | ((p >= 144) & (p < 160)), 1.0, 0.0)
     return one, two
 
 
@@ -85,7 +80,8 @@
     assert n_sub == 4
     units = n_sub * nz
     rows_total = tok.shape[0]
-    part = WIDE // nctx
+    owners = st.shape[0]
+    part = PACKED // owners
     b = lax.axis_index("ctx")
     head = lax.axis_index("head")
     z = head // 2
@@ -303,7 +299,7 @@
 
     lax.fori_loop(1, nctx, start_doc, 0)
 
-    one_k, two_k = factor_bias((WIDE, 1), 0)
+    one_k, two_k = factor_bias((PACKED, 1), 0)
 
     def finish(i):
         rows = sub_rows(i)
@@ -314,9 +310,9 @@
         vcat[late, :] = v
         keeps = docr[0:1, late] == last_doc
         for j in range(2):
-            at = 256 + 512 * j
-            left = dot_nt(table[at : at + 256, 0:64], x) + one_k
-            right = dot_nt(table[at + 256 : at + 512, 0:64], x) + two_k
+            at = 256 + 2 * PACKED * j
+            left = dot_nt(table[at : at + PACKED, 0:64], x) + one_k
+            right = dot_nt(table[at + PACKED : at + 2 * PACKED, 0:64], x) + two_k
             phi_k = jnp.where(keeps, left * right, 0.0).astype(BF16)
             st_acc[j] += dot(phi_k, v[:, j * 128 : (j + 1) * 128])
 
@@ -357,7 +353,7 @@
         )
 
     for j in range(2):
-        st_send[:, j * part : (j + 1) * part, :] = st_acc[j].astype(BF16).reshape(nctx, part, 128)
+        st_send[:, j * part : (j + 1) * part, :] = st_acc[j].astype(BF16).reshape(owners, part, 128)
 
     def st_copy(c, slot):
         return pltpu.make_async_remote_copy(
@@ -369,8 +365,13 @@
             device_id_type=MESH,
         )
 
+    def start_state(c):
+        @pl.when(c < owners)
+        def _():
+            st_copy(c, b).start()
+
     for n in far_first:
-        st_copy(lax.rem(b + n, nctx), b).start()
+        start_state(lax.rem(b + n, nctx))
 
     def window_rows(i, carry):
         rows = sub_rows(i)
@@ -399,7 +400,7 @@
         rows = sub_rows(i)
         x = feat[rows, :]
         for j in range(2):
-            at = 1280 + 64 * j
+            at = 896 + 64 * j
             fq[j, rows, :] = dot(x, table[at : at + 64, 0:64]).astype(BF16)
         return carry
 
@@ -431,23 +432,24 @@
         )
 
     bulk(docs.at[0 : nctx - 1], doc_recv).wait()
-    bulk(st_recv.at[0 : nctx - 1], st_rsem).wait()
     docs[b] = doc[...]
-    st_recv[b] = st_send[b]
-
-    sums = jnp.zeros((2 * part, 128), F32)
-    for c in range(nctx - 1):
-        same = docs[c][7:8, 127:128] == docs[max(c - 1, 0)][7:8, 127:128]
-        sums = st_recv[c].astype(F32) + jnp.where(same, sums, 0.0)
-        st_sums[c + 1] = sums.astype(BF16)
 
     def start_sum(c):
         @pl.when(c > 0)
         def _():
             sum_back(c, b).start()
 
-    for n in far_first:
-        start_sum(lax.rem(b + n, nctx))
+    @pl.when(b < owners)
+    def _():
+        bulk(st_recv.at[0 : nctx - 1], st_rsem).wait()
+        st_recv[b] = st_send[b]
+        sums = jnp.zeros((2 * part, 128), F32)
+        for c in range(nctx - 1):
+            same = docs[c][7:8, 127:128] == docs[max(c - 1, 0)][7:8, 127:128]
+            sums = st_recv[c].astype(F32) + jnp.where(same, sums, 0.0)
+            st_sums[c + 1] = sums.astype(BF16)
+        for n in far_first:
+            start_sum(lax.rem(b + n, nctx))
 
     one_q, two_q = factor_bias((1, WIDE), 1)
 
@@ -493,13 +495,19 @@
     def _():
         st[...] = jnp.zeros_like(st)
 
-    @pl.when(b > 0)
-    def _():
-        bulk(st.at[0 : nctx - 1], sum_rsem).wait()
+    @pl.when((b > 0) & (b < owners))
+    def _():
+        bulk(st.at[0 : owners - 1], sum_rsem).wait()
         st[b] = st_sums[b]
 
+    @pl.when((b > 0) & (b >= owners))
+    def _():
+        bulk(st, sum_rsem).wait()
+
+    rest = jnp.zeros((WIDE - PACKED, 128), BF16)
     state = [
-        st[:, j * part : (j + 1) * part, :].reshape(WIDE, 128) for j in range(2)
+        jnp.concatenate([st[:, j * part : (j + 1) * part, :].reshape(PACKED, 128), rest], 0)
+        for j in range(2)
     ]
 
     def mix_copy(i, side):
@@ -597,15 +605,22 @@
     bulk(gath.at[k], par_send).wait()
     bulk(sbuf, rs_send).wait()
     bulk(docs.at[0 : nctx - 1], doc_send).wait()
-    bulk(st_send.at[0 : nctx - 1], st_ssem).wait()
     bulk(mix.at[k], mix_send).wait()
     bulk(wo.at[k], wo_send).wait()
 
+    @pl.when(b < owners)
+    def _():
+        bulk(st_send.at[0 : owners - 1], st_ssem).wait()
+
+    @pl.when(b >= owners)
+    def _():
+        bulk(st_send, st_ssem).wait()
+
     @pl.when(b == 0)
     def _():
         bulk(st_sums.at[0 : nctx - 1], sum_ssem).wait()
 
-    @pl.when(b > 0)
+    @pl.when((b > 0) & (b < owners))
     def _():
         bulk(st_sums.at[0 : nctx - 2], sum_ssem).wait()
 
@@ -624,6 +639,7 @@
         width = w_value.shape[0]
         n_sub = rows // SUB
         units = n_sub * nz
+        owners = min(nctx, 10)
         dma = pltpu.SemaphoreType.DMA
         vmem = pltpu.VMEM
         hbm_space = pl.BlockSpec(memory_space=pltpu.HBM)
@@ -654,11 +670,11 @@
                 vmem((nctx, 8, 128), jnp.int32),
                 vmem((rows, 256), F32),
                 vmem((rows, 256), F32),
-                vmem((2, WIDE, 128), F32),
-                vmem((nctx, 2 * WIDE // nctx, 128), BF16),
-                vmem((nctx, 2 * WIDE // nctx, 128), BF16),
-                vmem((nctx, 2 * WIDE // nctx, 128), BF16),
-                vmem((nctx, 2 * WIDE // nctx, 128), BF16),
+                vmem((2, PACKED, 128), F32),
+                vmem((owners, 2 * PACKED // owners, 128), BF16),
+                vmem((nctx, 2 * PACKED // owners, 128), BF16),
+                vmem((nctx, 2 * PACKED // owners, 128), BF16),
+                vmem((owners, 2 * PACKED // owners, 128), BF16),
                 vmem((2, rows, 256), BF16),
                 vmem((2, nz, 256, 256), BF16),
                 vmem((nz - 1, n_sub, SUB, 256), BF16),

time: 107 us -> 107 us (level)
  no operation moved by 1% of the time
where the time goes in v6:
time: 107 us
  Pallas kernels  106 us (99%)
    pallas_call x1, Pallas kernels, shards(): pl.pallas_call(functools.partial(kernel, nctx, nz), out_shape=jax.ShapeDt...  106 us

profile of v6, /device:TPU:2, one launch (start us, length us, event | category | flops | bytes accessed | tf_op | source)
XLA Modules:
  0.0 106.5 jit_solution(10015426843082910214)
XLA Ops:
  0.0 105.7 %based_layer.1 = bf16[1024,256]{1,0:T(8,128)(2,1)S(1)} custom-call(bf16[1024,256]{1,0:T(8,128)(2,1)} %tok.1, s32[8,128]{1,0:T(8,128)} %bitcast.3, bf16[64,4096]{1,0:T(8,128)(2,1)} %bitcast.2, bf16[4096,256]{1,0:T(8,128)(2,1)} %wv_in.1, bf16[4096,512]{1,0:T(8,128)(2,1)} %ww_in.1, bf16[256,4096]{1,0:T(8,128)(2,1)} %wo_in.1, ...), custom_call_target="tpu_custom_call" | custom-call | tf_op jit(solution)/shard_map/based_layer/pallas_call | solution.py:647
  105.7 0.8 copy.9

commit v7 on v6

--- a/solution.py
+++ b/solution.py
@@ -464,6 +464,7 @@
 
     lax.fori_loop(0, n_sub, query_rows, 0)
     taylor_rows(2)
+    taylor_rows(3)
 
     @pl.when(b == 0)
     def _():
@@ -584,10 +585,6 @@
         return carry
 
     def first_step(i, carry):
-        @pl.when(i == n_sub - 1)
-        def _():
-            taylor_rows(n_sub - 1)
-
         @pl.when(i < n_sub)
         def _():
             mix_rows(i, 0)

time: 107 us -> 108 us (level)
  no operation moved by 1% of the time
where the time goes in v7:
time: 108 us; the launch traced here: 107 us
  Pallas kernels  106 us (98%)
    pallas_call x1, Pallas kernels, shards(): pl.pallas_call(functools.partial(kernel, nctx, nz), out_shape=jax.ShapeDt...  106 us

profile of v7, /device:TPU:2, one launch (start us, length us, event | category | flops | bytes accessed | tf_op | source)
XLA Modules:
  0.0 106.5 jit_solution(5835596532541752359)
XLA Ops:
  0.0 105.7 %based_layer.1 = bf16[1024,256]{1,0:T(8,128)(2,1)S(1)} custom-call(bf16[1024,256]{1,0:T(8,128)(2,1)} %tok.1, s32[8,128]{1,0:T(8,128)} %bitcast.3, bf16[64,4096]{1,0:T(8,128)(2,1)} %bitcast.2, bf16[4096,256]{1,0:T(8,128)(2,1)} %wv_in.1, bf16[4096,512]{1,0:T(8,128)(2,1)} %ww_in.1, bf16[256,4096]{1,0:T(8,128)(2,1)} %wo_in.1, ...), custom_call_target="tpu_custom_call" | custom-call | tf_op jit(solution)/shard_map/based_layer/pallas_call | solution.py:644
  105.7 0.8 copy.9
